TPU v7x, 256 devices: a whole 4x4x8 slice. The times are simulated.
256 devices in a mesh: dom: 64 (over z, y, core), st: 4 (over x).
Axes of the slice: x: 4, y: 4, z: 8, core: 2. Of those that a mesh axis runs over, the one named last changes fastest.
Arguments:
- orbitals: float32 [64, 512, 32, 128], P('st', 'dom'), may hold values from -6 to 6
- levels: float32 [64], P('st'), may hold values from -2 to -0.5
- potential: float32 [512, 32, 128], P('dom'), may hold values from 0 to 2
- perturbation: float32 [512, 32, 128], P('dom'), may hold values from -3 to 3
- projector: float32 [526336], P('dom'), may hold values from -1.5 to 1.5
- point_cell: int32 [526336], P('dom'), may hold values from 0 to 32767, as said below
- point_atom: int32 [526336], P('dom'), may hold values from -1 to 1023, as said below
- kb_energy: float32 [1024], replicated, may hold values from 1 to 4
Outputs:
- response: float32 [64, 512, 32, 128], P('st', 'dom')
- density: float32 [512, 32, 128], P('dom', 'st')
Inputs may be any that keep to these rules, and one draw needn't show every extreme that they name: `point_cell`: within the domain's block of 8 x 32 x 128 cells in row-major order; 0 in unused slots. `point_atom`: -1 marks an unused slot, and a domain's unused slots come after its used ones; atom a has its centre in domain a // 16, and its slots lie in that domain or in the two beside it; no two used slots of a domain share both cell and atom.
All inputs are finite; a program needn't handle non-finite values.
Results may differ from a plain program's by a relative error of at most 0.0001.
Values sent between devices are 32-bit elements; how exact they have to be, the bound alone decides.
A program may use at most 128 MiB of HBM per device.

v0:
```python
import jax
import jax.numpy as jnp
from jax import lax
from jax.sharding import PartitionSpec as P

ATOM_DEV = 16
ITERS = 4


STENCIL = (
    -5369.0 / 1800.0,
    12.0 / 7.0,
    -15.0 / 56.0,
    10.0 / 189.0,
    -1.0 / 112.0,
    2.0 / 1925.0,
    -1.0 / 16632.0,
)
HIGHEST = lax.Precision.HIGHEST


def with_halo(block, sides, width):
    for axis, dim in sides:
        count = lax.axis_size(axis)
        forward = [(i, i + 1) for i in range(count - 1)]
        backward = [(target, source) for source, target in forward]
        low = lax.ppermute(
            lax.slice_in_dim(block, block.shape[dim] - width, None, axis=dim), axis, forward
        )
        high = lax.ppermute(lax.slice_in_dim(block, 0, width, axis=dim), axis, backward)
        block = jnp.concatenate([low, block, high], axis=dim)
    return block


def sent_to_all(shard, axis):
    count = lax.axis_size(axis)
    return lax.all_to_all(
        jnp.broadcast_to(shard[None], (count, *shard.shape)), axis, 0, 0, tiled=True
    )


def of_everyone(shard, axis):
    return sent_to_all(shard, axis).sum(axis=0)


def together(arrays, axis):
    ends = [0]
    for a in arrays:
        ends.append(ends[-1] + a.size)
    total = of_everyone(jnp.concatenate([a.ravel() for a in arrays]), axis)
    return tuple((total[b:e].reshape(a.shape) for a, b, e in zip(arrays, ends, ends[1:])))


def cut_along(shard, dim, count):
    lengths = shard.shape
    tiles = shard.reshape(*lengths[:dim], count, lengths[dim] // count, *lengths[dim + 1 :])
    return jnp.moveaxis(tiles, dim, 0)


def summed_on_arrival(shard, axis, dim):
    count = lax.axis_size(axis)
    tiles = lax.all_to_all(cut_along(shard, dim, count), axis, 0, 0, tiled=True)
    return jnp.sum(tiles, axis=0)


def laplace(field, extended):
    width, height, depth = (field.shape[1], field.shape[2], field.shape[3])
    beside_all = jnp.pad(field, ((0, 0), (0, 0), (6, 6), (6, 6)))
    result = 3.0 * STENCIL[0] * field
    for shift in range(1, 7):
        lower = 6 - shift
        upper = 6 + shift
        beside = (
            extended[:, upper : upper + width]
            + extended[:, lower : lower + width]
            + beside_all[:, :, upper : upper + height, 6 : 6 + depth]
            + beside_all[:, :, lower : lower + height, 6 : 6 + depth]
            + beside_all[:, :, 6 : 6 + height, upper : upper + depth]
            + beside_all[:, :, 6 : 6 + height, lower : lower + depth]
        )
        result = result + STENCIL[shift] * beside
    return result


def atom_totals(partial_value, group):
    gathered = with_halo(partial_value, (("dom", 1),), group)
    owned = (
        gathered[:, :group]
        + gathered[:, 2 * group : 3 * group]
        + gathered[:, 4 * group : 5 * group]
    )
    return with_halo(owned, (("dom", 1),), group)


def inner(left, right):
    return jnp.sum(left * right, axis=(1, 2, 3))


def expand(values):
    return values[:, None, None, None]


def paired(residual, image):
    return together((inner(residual, residual), inner(residual, image)), "dom")


def shards(orbitals, levels, potential, perturbation, projector, point_cell, point_atom, kb_energy):
    index = lax.axis_index("dom")
    group = ATOM_DEV
    block = orbitals.shape[0]
    slots = jnp.where(point_atom >= 0, point_atom - (index - 1) * group, -1)
    member = (slots[:, None] == jnp.arange(3 * group, dtype=jnp.int32)[None, :]).astype(jnp.float32)
    energies = lax.dynamic_slice_in_dim(
        jnp.pad(kb_energy, (group, group)), index * group, 3 * group
    )
    shifted = potential[None] - expand(levels)

    def operate(field):
        extended = with_halo(field, (("dom", 1),), 6)
        flat = field.reshape(block, -1)
        picked = flat[:, point_cell] * projector[None, :]
        partial_value = jnp.dot(picked, member, precision=HIGHEST)
        coeffs = atom_totals(partial_value, group) * energies[None, :]
        spread = jnp.dot(coeffs, member.T, precision=HIGHEST) * projector[None, :]
        projected = jnp.zeros_like(flat).at[:, point_cell].add(spread).reshape(field.shape)
        return -0.5 * laplace(field, extended) + shifted * field + projected

    right = -perturbation[None] * orbitals
    solution = jnp.zeros_like(right)
    residual = right
    image = operate(residual)
    norm_now, product = paired(residual, image)
    alpha = norm_now / product
    direction, along = (residual, image)
    for turn in range(ITERS):
        solution = solution + expand(alpha) * direction
        residual = residual - expand(alpha) * along
        if turn + 1 < ITERS:
            image = operate(residual)
            norm_next, product = paired(residual, image)
            ratio = norm_next / norm_now
            alpha = norm_next / (product - ratio * norm_next / alpha)
            direction = residual + expand(ratio) * direction
            along = image + expand(ratio) * along
            norm_now = norm_next
    density = summed_on_arrival(4.0 * jnp.sum(orbitals * solution, axis=0), "st", 1)
    return (solution, density)


def solution(mesh):
    in_specs = (
        P("st", "dom", None, None),
        P("st"),
        P("dom", None, None),
        P("dom", None, None),
        P("dom"),
        P("dom"),
        P("dom"),
        P(),
    )
    out_specs = (P("st", "dom", None, None), P("dom", "st", None))
    return jax.shard_map(shards, mesh=mesh, in_specs=in_specs, out_specs=out_specs, check_vma=False)
```

profile of v0, /device:TPU:1, one launch (start us, length us, event | category | flops | bytes accessed | tf_op | source)
XLA Modules:
  0.0 772.7 jit_solution(13451617784116764342)
XLA Ops:
  5.6 5.1 collective-permute-start
  12.7 8.6 %copy.60 = f32[16,8,32,128]{0,3,2,1:T(8,128)} copy(f32[16,8,32,128]{3,2,1,0:T(8,128)S(1)} %broadcast_multiply_fusion) | data formatting | bytes 4194304 | tf_op jit(solution)/shard_map/mul | solution.py:128
  21.4 22.0 %gather_fusion = f32[8224,16]{1,0:T(8,128)} fusion(f32[16,32768]{0,1:T(8,128)} %bitcast.24, s32[9216]{0:T(1024)S(1)} %pad_clamp_fusion), kind=kCustom, calls=%fused_computation | custom fusion | bytes 1085568 | tf_op jit(solution)/shard_map/gather | solution.py:121
  43.4 7.9 %fusion.18 = f32[16,48]{1,0:T(8,128)S(1)} fusion(f32[8224,16]{1,0:T(8,128)} %gather_fusion, f32[8224]{0:T(1024)S(1)} %copy-done.2, s32[8224]{0:T(1024)S(1)} %subtract_select_fusion), kind=kOutput, calls=%fused_computation.210 | convolution fusion | flops 76318720 | bytes 595200 | tf_op jit(solution)/shard_map/dot_general | solution.py:122
  53.3 3.0 collective-permute-start.3
  65.9 2.7 copy.61
  68.6 61.1 %scatter_custom_fusion = f32[16,32768]{0,1:T(8,128)} fusion(s32[8224]{0:T(1024)S(1)} %compare_select_fusion, f32[8224,16]{1,0:T(8,128)} %copy.61, f32[]{:T(128)} %constant.17.clone.1), kind=kCustom, calls=%fused_computation.118 | custom fusion | flops 131584 | bytes 2097664 | tf_op jit(solution)/shard_map/scatter-add | solution.py:125
  129.7 11.0 %copy.62 = f32[16,8,32,128]{3,2,1,0:T(8,128)} copy(f32[16,8,32,128]{0,3,2,1:T(8,128)} %bitcast.21) | data formatting | bytes 4194304 | tf_op jit(solution)/shard_map/reshape | solution.py:125
  140.7 10.8 %multiply_reduce_fusion.7 = (f32[16]{0:T(128)S(1)}, f32[16]{0:T(128)S(1)}, f32[16,8,32,128]{3,2,1,0:T(8,128)}) fusion(f32[16,8,32,128]{3,2,1,0:T(8,128)S(1)} %broadcast_multiply_fusion, f32[16,8,32,128]{3,2,1,0:T(8,128)} %copy.62, f32[16]{0:T(128)S(1)} %copy-done.6, f32[8,32,128]{2,1,0:T(8,128)S(1)} %copy-done.3, ...), kind=kLoop, calls=%fused_computation.458 | loop fusion | flops 33554400 | bytes 9568448 | tf_op jit(solution)/shard_map/reduce_sum | solution.py:96
  151.6 26.8 %all_to_all.29 = f32[64,1,32]{2,1,0:T(1,128)S(1)} all-to-all(f32[64,1,32]{2,1,0:T(1,128)S(1)} %broadcast_in_dim.16), channel_id=1, replica_groups=mesh['dom'=64,'st'=4] {'dom'}, dimensions={0} | all-to-all | bytes 16384 | tf_op jit(solution)/shard_map/all_to_all | solution.py:37
  178.6 2.9 multiply_subtract_fusion.2
  183.6 2.6 collective-permute-start.6
  186.2 3.0 collective-permute-start.7
  189.2 8.6 %copy.64 = f32[16,8,32,128]{0,3,2,1:T(8,128)} copy(f32[16,8,32,128]{3,2,1,0:T(8,128)S(1)} %multiply_subtract_fusion.2) | data formatting | bytes 4194304 | tf_op jit(solution)/shard_map/sub | solution.py:137
  197.8 22.0 %gather_fusion.1 = f32[8224,16]{1,0:T(8,128)} fusion(f32[16,32768]{0,1:T(8,128)} %bitcast.26, s32[9216]{0:T(1024)S(1)} %pad_clamp_fusion), kind=kCustom, calls=%fused_computation.1 | custom fusion | bytes 1085568 | tf_op jit(solution)/shard_map/gather | solution.py:121
  219.8 7.9 %fusion.16 = f32[16,48]{1,0:T(8,128)S(1)} fusion(f32[8224,16]{1,0:T(8,128)} %gather_fusion.1, f32[8224]{0:T(1024)S(1)} %copy-done.2, s32[8224]{0:T(1024)S(1)} %subtract_select_fusion), kind=kOutput, calls=%fused_computation.208 | convolution fusion | flops 76318720 | bytes 595200 | tf_op jit(solution)/shard_map/dot_general | solution.py:122
  239.0 2.6 collective-permute-done.11
  242.2 2.7 copy.65
  244.9 61.5 %scatter_custom_fusion.1 = f32[16,32768]{0,1:T(8,128)} fusion(s32[8224]{0:T(1024)S(1)} %compare_select_fusion, f32[8224,16]{1,0:T(8,128)} %copy.65, f32[]{:T(128)} %constant.17.clone.1), kind=kCustom, calls=%fused_computation.116 | custom fusion | flops 131584 | bytes 2097664 | tf_op jit(solution)/shard_map/scatter-add | solution.py:125
  306.4 11.1 %copy.66 = f32[16,8,32,128]{3,2,1,0:T(8,128)} copy(f32[16,8,32,128]{0,3,2,1:T(8,128)} %bitcast.22) | data formatting | bytes 4194304 | tf_op jit(solution)/shard_map/reshape | solution.py:125
  317.5 11.0 %multiply_reduce_fusion.5 = (f32[16]{0:T(128)S(1)}, f32[16]{0:T(128)S(1)}, f32[16,8,32,128]{3,2,1,0:T(8,128)}) fusion(f32[16,8,32,128]{3,2,1,0:T(8,128)S(1)} %multiply_subtract_fusion.2, f32[16,8,32,128]{3,2,1,0:T(8,128)} %copy.66, f32[16]{0:T(128)S(1)} %copy-done.6, f32[8,32,128]{2,1,0:T(8,128)S(1)} %copy-done.3, ...), kind=kLoop, calls=%fused_computation.455 | loop fusion | flops 33554400 | bytes 9568448 | tf_op jit(solution)/shard_map/reduce_sum | solution.py:96
  328.6 21.3 %all_to_all.30 = f32[64,1,32]{2,1,0:T(1,128)S(1)} all-to-all(f32[64,1,32]{2,1,0:T(1,128)S(1)} %broadcast_in_dim.17), channel_id=1, replica_groups=mesh['dom'=64,'st'=4] {'dom'}, dimensions={0} | all-to-all | bytes 16384 | tf_op jit(solution)/shard_map/all_to_all | solution.py:37
  350.1 3.1 multiply_subtract_fusion.1
  355.5 2.6 collective-permute-start.12
  358.1 3.0 collective-permute-start.13
  361.1 10.0 %copy.68 = f32[16,8,32,128]{0,3,2,1:T(8,128)} copy(f32[16,8,32,128]{3,2,1,0:T(8,128)} %copy-done) | data formatting | bytes 4194304 | tf_op jit(solution)/shard_map/sub | solution.py:137
  371.1 22.0 %gather_fusion.2 = f32[8224,16]{1,0:T(8,128)} fusion(f32[16,32768]{0,1:T(8,128)} %bitcast.27, s32[9216]{0:T(1024)S(1)} %pad_clamp_fusion), kind=kCustom, calls=%fused_computation.2 | custom fusion | bytes 1085568 | tf_op jit(solution)/shard_map/gather | solution.py:121
  393.1 7.9 %fusion.14 = f32[16,48]{1,0:T(8,128)S(1)} fusion(f32[8224,16]{1,0:T(8,128)} %gather_fusion.2, f32[8224]{0:T(1024)S(1)} %copy-done.2, s32[8224]{0:T(1024)S(1)} %subtract_select_fusion), kind=kOutput, calls=%fused_computation.206 | convolution fusion | flops 76318720 | bytes 595200 | tf_op jit(solution)/shard_map/dot_general | solution.py:122
  410.0 2.5 collective-permute-start.17
  415.6 2.7 copy.69
  418.3 61.1 %scatter_custom_fusion.2 = f32[16,32768]{0,1:T(8,128)} fusion(s32[8224]{0:T(1024)S(1)} %compare_select_fusion, f32[8224,16]{1,0:T(8,128)} %copy.69, f32[]{:T(128)} %constant.17.clone.1), kind=kCustom, calls=%fused_computation.114 | custom fusion | flops 131584 | bytes 2097664 | tf_op jit(solution)/shard_map/scatter-add | solution.py:125
  479.4 11.0 %copy.70 = f32[16,8,32,128]{3,2,1,0:T(8,128)} copy(f32[16,8,32,128]{0,3,2,1:T(8,128)} %bitcast.23) | data formatting | bytes 4194304 | tf_op jit(solution)/shard_map/reshape | solution.py:125
  490.4 39.7 %multiply_reduce_fusion.3 = (f32[16]{0:T(128)S(1)}, f32[16]{0:T(128)S(1)}, f32[16,8,32,128]{3,2,1,0:T(8,128)}) fusion(f32[16,8,32,128]{3,2,1,0:T(8,128)} %copy-done, f32[16,8,32,128]{3,2,1,0:T(8,128)} %copy.70, f32[16]{0:T(128)S(1)} %copy-done.6, f32[8,32,128]{2,1,0:T(8,128)S(1)} %copy-done.3, f32[16,6,32,128]{3,2,1,0:T(8,128)} %collective-permute-done.13, ...), kind=kLoop, calls=%fused_computation.451 | loop fusion | flops 33554400 | bytes 9568448 | tf_op jit(solution)/shard_map/reduce_sum | solution.py:96
  530.1 21.3 %all_to_all.31 = f32[64,1,32]{2,1,0:T(1,128)S(1)} all-to-all(f32[64,1,32]{2,1,0:T(1,128)S(1)} %broadcast_in_dim.18), channel_id=1, replica_groups=mesh['dom'=64,'st'=4] {'dom'}, dimensions={0} | all-to-all | bytes 16384 | tf_op jit(solution)/shard_map/all_to_all | solution.py:37
  551.6 4.6 multiply_subtract_fusion
  558.7 2.6 collective-permute-start.18
  561.3 3.2 collective-permute-start.19
  564.5 10.0 %copy.72 = f32[16,8,32,128]{0,3,2,1:T(8,128)} copy(f32[16,8,32,128]{3,2,1,0:T(8,128)} %copy-done.1) | data formatting | bytes 4194304 | tf_op jit(solution)/shard_map/sub | solution.py:137
  574.5 22.0 %gather_fusion.3 = f32[8224,16]{1,0:T(8,128)} fusion(f32[16,32768]{0,1:T(8,128)} %bitcast.25, s32[9216]{0:T(1024)S(1)} %pad_clamp_fusion), kind=kCustom, calls=%fused_computation.3 | custom fusion | bytes 1085568 | tf_op jit(solution)/shard_map/gather | solution.py:121
  596.4 7.9 %fusion.12 = f32[16,48]{1,0:T(8,128)S(1)} fusion(f32[8224,16]{1,0:T(8,128)} %gather_fusion.3, f32[8224]{0:T(1024)S(1)} %copy-done.2, s32[8224]{0:T(1024)S(1)} %subtract_select_fusion), kind=kOutput, calls=%fused_computation.204 | convolution fusion | flops 76318720 | bytes 595200 | tf_op jit(solution)/shard_map/dot_general | solution.py:122
  615.7 2.6 collective-permute-done.23
  618.9 2.7 copy.73
  621.6 61.1 %scatter_custom_fusion.3 = f32[16,32768]{0,1:T(8,128)} fusion(s32[8224]{0:T(1024)S(1)} %compare_select_fusion, f32[8224,16]{1,0:T(8,128)} %copy.73, f32[]{:T(128)} %constant.17.clone.1), kind=kCustom, calls=%fused_computation.112 | custom fusion | flops 131584 | bytes 2097664 | tf_op jit(solution)/shard_map/scatter-add | solution.py:125
  682.7 11.0 %copy.74 = f32[16,8,32,128]{3,2,1,0:T(8,128)} copy(f32[16,8,32,128]{0,3,2,1:T(8,128)} %bitcast.20) | data formatting | bytes 4194304 | tf_op jit(solution)/shard_map/reshape | solution.py:125
  693.7 41.7 %multiply_reduce_fusion.1 = (f32[16]{0:T(128)S(1)}, f32[16]{0:T(128)S(1)}) fusion(f32[16,8,32,128]{3,2,1,0:T(8,128)} %copy-done.1, f32[16,8,32,128]{3,2,1,0:T(8,128)} %copy.74, f32[16]{0:T(128)S(1)} %copy-done.6, f32[8,32,128]{2,1,0:T(8,128)S(1)} %copy-done.3, f32[16,6,32,128]{3,2,1,0:T(8,128)} %collective-permute-done.19, ...), kind=kLoop, calls=%fused_computation.448 | loop fusion | flops 33554400 | bytes 7471296 | tf_op jit(solution)/shard_map/reduce_sum | solution.py:96
  735.5 21.6 %all_to_all.32 = f32[64,1,32]{2,1,0:T(1,128)S(1)} all-to-all(f32[64,1,32]{2,1,0:T(1,128)S(1)} %broadcast_in_dim.19), channel_id=1, replica_groups=mesh['dom'=64,'st'=4] {'dom'}, dimensions={0} | all-to-all | bytes 16384 | tf_op jit(solution)/shard_map/all_to_all | solution.py:37
  757.3 5.7 multiply_reduce_fusion
  763.0 8.6 %all_to_all.33 = f32[4,8,8,128]{3,2,1,0:T(8,128)S(1)} all-to-all(f32[4,8,8,128]{3,2,1,0:T(8,128)S(1)} %copy.76), channel_id=1, replica_groups=mesh['dom'=64,'st'=4] {'st'}, dimensions={0} | all-to-all | bytes 262144 | tf_op jit(solution)/shard_map/all_to_all | solution.py:62
  (94 shorter events, 63.0 us)
Async XLA Ops:
  5.6 135.1 %collective-permute-start = (f32[16,6,32,128]{3,2,1,0:T(8,128)}, f32[16,6,32,128]{3,2,1,0:T(8,128)}, u32[]{:S(2)}, u32[]{:S(2)}) collective-permute-start(f32[16,6,32,128]{3,2,1,0:T(8,128)} %get-tuple-element.29), channel_id=1, source_target_pairs={{4,0},{8,4},{12,8},{16,12},{20,16},{24,20},{28,24},{32,28},{36,32}... | collective-permute-start | bytes 4718600 | tf_op jit(solution)/shard_map/ppermute | solution.py:30
  10.8 10.6 %copy-start.4 = (s32[8224]{0:T(1024)S(1)}, s32[8224]{0:T(1024)}, u32[]{:S(2)}) copy-start(s32[8224]{0:T(1024)} %param.13) | copy-start | bytes 98692
  10.8 129.9 %collective-permute-start.1 = (f32[16,6,32,128]{3,2,1,0:T(8,128)}, f32[16,6,32,128]{3,2,1,0:T(8,128)}, u32[]{:S(2)}, u32[]{:S(2)}) collective-permute-start(f32[16,6,32,128]{3,2,1,0:T(8,128)} %get-tuple-element.30), channel_id=1, source_target_pairs={{0,4},{4,8},{8,12},{12,16},{16,20},{20,24},{24,28},{28,32},{32,36}... | collective-permute-start | bytes 4718600 | tf_op jit(solution)/shard_map/ppermute | solution.py:27
  21.3 22.0 %copy-start.5 = (s32[8224]{0:T(1024)S(1)}, s32[8224]{0:T(1024)}, u32[]{:S(2)}) copy-start(s32[8224]{0:T(1024)} %param.14) | copy-start | bytes 98692
  21.4 22.0 %copy-start.2 = (f32[8224]{0:T(1024)S(1)}, f32[8224]{0:T(1024)}, u32[]{:S(2)}) copy-start(f32[8224]{0:T(1024)} %param.12) | copy-start | bytes 98692
  43.4 19.3 %copy-start.7 = (f32[1024]{0:T(1024)S(1)}, f32[1024]{0:T(1024)}, u32[]{:S(2)}) copy-start(f32[1024]{0:T(1024)} %param.15) | copy-start | bytes 12292
  51.4 4.9 collective-permute-start.2
  53.3 5.0 collective-permute-start.3
  58.3 4.4 collective-permute-start.4
  60.3 5.0 collective-permute-start.5
  129.7 11.0 %copy-start.3 = (f32[8,32,128]{2,1,0:T(8,128)S(1)}, f32[8,32,128]{2,1,0:T(8,128)}, u32[]{:S(2)}) copy-start(f32[8,32,128]{2,1,0:T(8,128)} %param.10) | copy-start | bytes 393220
  129.7 11.0 %copy-start.6 = (f32[16]{0:T(128)S(1)}, f32[16]{0:T(128)}, u32[]{:S(2)}) copy-start(f32[16]{0:T(128)} %param.9) | copy-start | bytes 196
  183.6 133.9 %collective-permute-start.6 = (f32[16,6,32,128]{3,2,1,0:T(8,128)}, f32[16,6,32,128]{3,2,1,0:T(8,128)}, u32[]{:S(2)}, u32[]{:S(2)}) collective-permute-start(f32[16,6,32,128]{3,2,1,0:T(8,128)} %get-tuple-element.27), channel_id=1, source_target_pairs={{4,0},{8,4},{12,8},{16,12},{20,16},{24,20},{28,24},{32,28},{36,32}... | collective-permute-start | bytes 4718600 | tf_op jit(solution)/shard_map/ppermute | solution.py:30
  186.2 131.3 %collective-permute-start.7 = (f32[16,6,32,128]{3,2,1,0:T(8,128)}, f32[16,6,32,128]{3,2,1,0:T(8,128)}, u32[]{:S(2)}, u32[]{:S(2)}) collective-permute-start(f32[16,6,32,128]{3,2,1,0:T(8,128)} %get-tuple-element.28), channel_id=1, source_target_pairs={{0,4},{4,8},{8,12},{12,16},{16,20},{20,24},{24,28},{28,32},{32,36}... | collective-permute-start | bytes 4718600 | tf_op jit(solution)/shard_map/ppermute | solution.py:27
  227.7 4.3 collective-permute-start.8
  229.6 5.0 collective-permute-start.9
  234.7 4.3 collective-permute-start.10
  236.6 5.0 collective-permute-start.11
  353.2 2.4 copy-start
  355.5 134.8 %collective-permute-start.12 = (f32[16,6,32,128]{3,2,1,0:T(8,128)}, f32[16,6,32,128]{3,2,1,0:T(8,128)}, u32[]{:S(2)}, u32[]{:S(2)}) collective-permute-start(f32[16,6,32,128]{3,2,1,0:T(8,128)} %get-tuple-element.25), channel_id=1, source_target_pairs={{4,0},{8,4},{12,8},{16,12},{20,16},{24,20},{28,24},{32,28},{36,32}... | collective-permute-start | bytes 4718600 | tf_op jit(solution)/shard_map/ppermute | solution.py:30
  358.1 132.2 %collective-permute-start.13 = (f32[16,6,32,128]{3,2,1,0:T(8,128)}, f32[16,6,32,128]{3,2,1,0:T(8,128)}, u32[]{:S(2)}, u32[]{:S(2)}) collective-permute-start(f32[16,6,32,128]{3,2,1,0:T(8,128)} %get-tuple-element.26), channel_id=1, source_target_pairs={{0,4},{4,8},{8,12},{12,16},{16,20},{20,24},{24,28},{28,32},{32,36}... | collective-permute-start | bytes 4718600 | tf_op jit(solution)/shard_map/ppermute | solution.py:27
  401.1 4.3 collective-permute-start.14
  403.0 5.0 collective-permute-start.15
  408.0 4.5 collective-permute-start.16
  410.0 5.0 collective-permute-start.17
  556.2 2.4 copy-start.1
  558.7 135.0 %collective-permute-start.18 = (f32[16,6,32,128]{3,2,1,0:T(8,128)}, f32[16,6,32,128]{3,2,1,0:T(8,128)}, u32[]{:S(2)}, u32[]{:S(2)}) collective-permute-start(f32[16,6,32,128]{3,2,1,0:T(8,128)} %get-tuple-element.23), channel_id=1, source_target_pairs={{4,0},{8,4},{12,8},{16,12},{20,16},{24,20},{28,24},{32,28},{36,32}... | collective-permute-start | bytes 4718600 | tf_op jit(solution)/shard_map/ppermute | solution.py:30
  561.3 132.5 %collective-permute-start.19 = (f32[16,6,32,128]{3,2,1,0:T(8,128)}, f32[16,6,32,128]{3,2,1,0:T(8,128)}, u32[]{:S(2)}, u32[]{:S(2)}) collective-permute-start(f32[16,6,32,128]{3,2,1,0:T(8,128)} %get-tuple-element.24), channel_id=1, source_target_pairs={{0,4},{4,8},{8,12},{12,16},{16,20},{20,24},{24,28},{28,32},{32,36}... | collective-permute-start | bytes 4718600 | tf_op jit(solution)/shard_map/ppermute | solution.py:27
  604.4 4.3 collective-permute-start.20
  606.3 5.0 collective-permute-start.21
  611.4 4.3 collective-permute-start.22
  613.3 5.0 collective-permute-start.23
where the time goes:
time: 784 us; the launch traced here: 773 us
  other arithmetic  369 us (47%)
  local copies, waits for them, and re-layouts  190 us (24%)
  blocking collectives  99.7 us (13%)
  starting transfers between devices  59.2 us (8%)
  matrix products  34 us (4%)
  waiting for transfers between devices  19.7 us (3%)
    scatter-add x4, other arithmetic, operate(): jnp.zeros_like(flat).at[:, point_cell].add(spread).reshape(field.shape)  245 us
    reduce_sum x4, other arithmetic, inner(): return jnp.sum(left * right, axis=(1, 2, 3))  103 us
    all_to_all x4, blocking collectives, sent_to_all(): lax.all_to_all(jnp.broadcast_to(shard[None], (count, *shard.shape)), axis...  91 us
    gather x4, local copies, waits for them, and re-layouts, operate(): picked = flat[:, point_cell] * projector[None, :]  87.9 us
    reshape x4, local copies, waits for them, and re-layouts, operate(): jnp.zeros_like(flat).at[:, point_cell].add(spread).reshape(field.shape)  44.1 us
    ppermute x12, starting transfers between devices, with_halo(): lax.ppermute(lax.slice_in_dim(block, 0, width, axis=dim), axis, backward)  32.7 us
    dot_general x4, matrix products, operate(): partial_value = jnp.dot(picked, member, precision=HIGHEST)  31.5 us
    sub x3, local copies, waits for them, and re-layouts, shards(): residual = residual - expand(alpha) * along  28.6 us
  transfers between devices with their start and end apart: 24, of which 8 were waited for; matrix products, arithmetic and copies ran while one was open for 59% of the time, Pallas kernels for 0%

commit v1 on v0

v1 whole, which is shorter than its diff:
```python
import numpy as np
import jax
import jax.numpy as jnp
from jax import lax
from jax.experimental import pallas as pl
from jax.experimental.pallas import tpu as pltpu
from jax.sharding import PartitionSpec as P

ATOM_DEV = 16
SLOTS = 3 * ATOM_DEV
SX, NY, NZ = 8, 32, 128
HALO = 6
EXT = SX + 2 * HALO
NYP = NY + 2 * HALO
N_DOM = 64
PLANE = 8
DEPTH = 8
C = (
    -5369.0 / 1800.0,
    12.0 / 7.0,
    -15.0 / 56.0,
    10.0 / 189.0,
    -1.0 / 112.0,
    2.0 / 1925.0,
    -1.0 / 16632.0,
)
F32 = jnp.float32
BF16 = jnp.bfloat16
UNROLL = 8


def depth_matrix():
    lag = np.abs(np.arange(NZ)[:, None] - np.arange(NZ)[None, :])
    band = np.zeros((NZ, NZ), np.float32)
    for k in range(1, 7):
        band[lag == k] = -0.5 * C[k]
    high = band.astype(jnp.bfloat16)
    low = (band - high.astype(np.float32)).astype(jnp.bfloat16)
    half = np.concatenate([high, low], axis=1)
    return np.concatenate([half, half], axis=0)


def both_parts(value, axis):
    high = value.astype(BF16).astype(F32)
    return jnp.concatenate([high, value - high], axis=axis).astype(BF16)


def table_kernel(cell, atom, value, table, dense):
    first = (lax.axis_index("dom") - 1) * ATOM_DEV
    slots = cell.shape[0]

    def clear(i, _):
        dense[pl.ds(pl.multiple_of(i * 64, 64), 64), :] = jnp.zeros((64, NZ), F32)
        return 0

    lax.fori_loop(0, dense.shape[0] // 64, clear, 0)

    def halve(_, ends):
        low, high = ends
        mid = (low + high) // 2
        used = atom[jnp.minimum(mid, slots - 1)] >= 0
        go = low < high
        return (
            jnp.where(go & used, mid + 1, low),
            jnp.where(go & jnp.logical_not(used), mid, high),
        )

    used, _ = lax.fori_loop(0, 15, halve, (jnp.int32(0), jnp.int32(slots)))
    lanes = lax.broadcasted_iota(jnp.int32, (1, NZ), 1)

    def put(i, _):
        for u in range(UNROLL):
            s = i * UNROLL + u
            c = cell[s]
            a = atom[s] - first
            live = s < used
            row = jnp.where(live, (c >> 7) * SLOTS + a, 0)
            lane = jnp.where(live, c & 127, -1)
            pltpu.store(
                dense.at[pl.ds(row, 1), :],
                jnp.full((1, NZ), value[s], F32),
                mask=lanes == lane,
            )
        return 0

    lax.fori_loop(0, (used + UNROLL - 1) // UNROLL, put, 0)

    def split(i, _):
        table[i] = both_parts(dense[pl.ds(pl.multiple_of(i * SLOTS, SLOTS), SLOTS), :], 0)
        return 0

    lax.fori_loop(0, SX * NY, split, 0)


def build_table(projector, point_cell, point_atom):
    smem = pl.BlockSpec(memory_space=pltpu.SMEM)
    return pl.pallas_call(
        table_kernel,
        out_shape=jax.ShapeDtypeStruct((SX * NY, 2 * SLOTS, NZ), BF16),
        in_specs=[smem, smem, smem],
        out_specs=pl.BlockSpec(memory_space=pltpu.VMEM),
        scratch_shapes=[pltpu.VMEM((SX * NY * SLOTS, NZ), F32)],
        compiler_params=pltpu.CompilerParams(vmem_limit_bytes=40 * 2**20),
        cost_estimate=pl.CostEstimate(flops=0, bytes_accessed=40 * 2**20, transcendentals=0),
        name="projector_table",
    )(point_cell, point_atom, projector)


def solve_kernel(
    own_in, low_in, high_in, table_in, pot_in, lev, energy, tz,
    x_out,
    r, s, w, hb, hb2, hist, table, potb, st1, st2, pj, msg, pmsg, scal, tot, lhs,
    sem_in, h_send, h_recv, a_send, a_recv, b_send, b_recv, p_send, p_recv,
):
    d = lax.axis_index("dom")
    zi = d // PLANE
    ji = d % PLANE
    inner = pl.ds(HALO, NY)

    loads = []
    for g in range(2):
        loads += [
            pltpu.make_async_copy(own_in.at[:, g], r.at[g, pl.ds(HALO, SX), inner], sem_in.at[4 * g]),
            pltpu.make_async_copy(low_in.at[:, g], r.at[g, pl.ds(0, HALO), inner], sem_in.at[4 * g + 1]),
            pltpu.make_async_copy(high_in.at[:, g], r.at[g, pl.ds(HALO + SX, HALO), inner], sem_in.at[4 * g + 2]),
            pltpu.make_async_copy(own_in.at[:, g], hist.at[0, g], sem_in.at[4 * g + 3]),
        ]
    loads.append(pltpu.make_async_copy(table_in, table, sem_in.at[8]))
    for c in loads:
        c.start()

    zero = jnp.zeros((HALO, 8, NZ), F32)

    def clear(i, _):
        for g in range(2):
            r[g, i, pl.ds(0, HALO)] = zero
            r[g, i, pl.ds(HALO + NY, HALO)] = zero
        return 0

    lax.fori_loop(0, EXT, clear, 0)

    def clear_halo(base):
        plane = jnp.zeros((NY, 8, NZ), F32)

        def one(i, _):
            for k in range(2):
                for g in range(2):
                    hb[k, g, base + i] = plane
            for g in range(2):
                hb2[g, i] = plane
            return 0

        lax.fori_loop(0, HALO, one, 0)

    @pl.when(d == 0)
    def _():
        clear_halo(0)

    @pl.when(d == N_DOM - 1)
    def _():
        clear_halo(HALO)

    for k in range(4):
        for g in range(2):
            pj[k, g] = jnp.zeros((4, 8, NZ), F32)

    near = ((-2, d >= 2), (-1, d >= 1), (1, d < N_DOM - 1), (2, d < N_DOM - 2))

    def in_plane(i):
        return zi * PLANE + (ji + i) % PLANE

    def in_column(i):
        return ((zi + i) % DEPTH) * PLANE + ji

    barrier = pltpu.get_barrier_semaphore()
    count = jnp.int32(PLANE - 1 + DEPTH - 1)
    for i in range(1, PLANE):
        pl.semaphore_signal(barrier, inc=1, device_id={"dom": in_plane(i)})
    for i in range(1, DEPTH):
        pl.semaphore_signal(barrier, inc=1, device_id={"dom": in_column(i)})
    for step, there in near:
        count = count + there.astype(jnp.int32)

        @pl.when(there)
        def _(step=step):
            pl.semaphore_signal(barrier, inc=1, device_id={"dom": d + step})

    lanes = lax.broadcasted_iota(jnp.int32, (8, NZ), 1)

    def spread(i, _):
        rows = pot_in[pl.ds(pl.multiple_of(i * 8, 8), 8), :]
        for j in range(8):
            potb[i * 8 + j] = jnp.broadcast_to(rows[j : j + 1, :], (8, NZ))
        return 0

    lax.fori_loop(0, SX * NY // 8, spread, 0)
    pl.semaphore_wait(barrier, count)

    def project(blocks, row, acc):
        left = jnp.concatenate([both_parts(b, 0) for b in blocks], axis=1)
        right = jnp.concatenate([table[row + j] for j in range(len(blocks))], axis=1)
        return acc + lax.dot_general(
            left, right, (((1,), (1,)), ((), ())), preferred_element_type=F32
        )

    def near_copy(k, g, n):
        step = near[n][0]
        return pltpu.make_async_remote_copy(
            src_ref=pmsg.at[k, g],
            dst_ref=pj.at[k, g, 3 - n],
            send_sem=p_send.at[g, n],
            recv_sem=p_recv.at[k % 2, g, 3 - n],
            device_id={"dom": d + step},
        )

    def near_arrival(k, g, n):
        return pltpu.make_async_remote_copy(
            src_ref=pmsg.at[k, g],
            dst_ref=pj.at[k, g, n],
            send_sem=p_send.at[g, n],
            recv_sem=p_recv.at[k % 2, g, n],
            device_id={"dom": d + near[n][0]},
        )

    def send_projections(k, g, acc):
        part = acc[:8, :SLOTS] + acc[8:, :SLOTS] + acc[:8, SLOTS:] + acc[8:, SLOTS:]
        pmsg[k, g] = jnp.concatenate([part, jnp.zeros((8, NZ - SLOTS), F32)], axis=1)
        for n in range(4):

            @pl.when(near[n][1])
            def _(n=n):
                near_copy(k, g, n).start()

    def gathered_projections(k, g):
        for n in range(4):

            @pl.when(near[n][1])
            def _(n=n):
                near_arrival(k, g, n).wait_recv()
                near_copy(k, g, n).wait_send()

        total = pmsg[k, g]
        shifts = ((2 * ATOM_DEV, 0, 16), (ATOM_DEV, 0, 32), (-ATOM_DEV, 16, 48), (-2 * ATOM_DEV, 32, 48))
        for n, (back, low, high) in enumerate(shifts):
            moved = pltpu.roll(pj[k, g, n], (-back) % NZ, 1)
            total = total + jnp.where((lanes >= low) & (lanes < high), moved, 0.0)
        return total

    def plane_copy(k, g, i):
        return pltpu.make_async_remote_copy(
            src_ref=msg.at[k, g, 0],
            dst_ref=st1.at[k, g, ji],
            send_sem=a_send.at[g, i],
            recv_sem=a_recv.at[k % 2, g, i],
            device_id={"dom": in_plane(i)},
        )

    def plane_arrival(k, g, i):
        return pltpu.make_async_remote_copy(
            src_ref=msg.at[k, g, 0],
            dst_ref=st1.at[k, g, (ji + PLANE - i) % PLANE],
            send_sem=a_send.at[g, i],
            recv_sem=a_recv.at[k % 2, g, i],
            device_id={"dom": in_plane(i)},
        )

    def column_copy(k, g, i):
        return pltpu.make_async_remote_copy(
            src_ref=msg.at[k, g, 1],
            dst_ref=st2.at[k, g, zi],
            send_sem=b_send.at[g, i],
            recv_sem=b_recv.at[k % 2, g, i],
            device_id={"dom": in_column(i)},
        )

    def column_arrival(k, g, i):
        return pltpu.make_async_remote_copy(
            src_ref=msg.at[k, g, 1],
            dst_ref=st2.at[k, g, (zi + DEPTH - i) % DEPTH],
            send_sem=b_send.at[g, i],
            recv_sem=b_recv.at[k % 2, g, i],
            device_id={"dom": in_column(i)},
        )

    def send_sums(k, g, rr, rw):
        tile = jnp.where(
            lanes < 64, jnp.sum(rr, axis=1, keepdims=True), jnp.sum(rw, axis=1, keepdims=True)
        )
        msg[k, g, 0] = tile
        st1[k, g, ji] = tile
        for i in range(1, PLANE):
            plane_copy(k, g, i).start()

    def forward_sums(k, g):
        for i in range(1, PLANE):
            plane_arrival(k, g, i).wait_recv()
            plane_copy(k, g, i).wait_send()
        tile = st1[k, g, 0]
        for i in range(1, PLANE):
            tile = tile + st1[k, g, i]
        msg[k, g, 1] = tile
        st2[k, g, zi] = tile
        for i in range(1, DEPTH):
            column_copy(k, g, i).start()

    def take_sums(k, g):
        for i in range(1, DEPTH):
            column_arrival(k, g, i).wait_recv()
            column_copy(k, g, i).wait_send()
        tile = st2[k, g, 0]
        for i in range(1, DEPTH):
            tile = tile + st2[k, g, i]
        rr = jnp.broadcast_to(tile[:, 0:1], (8, NZ))
        rw = jnp.broadcast_to(tile[:, 64:65], (8, NZ))
        scal[g, 8 + k] = rr
        if k == 0:
            alpha, beta = rr / rw, jnp.zeros_like(rr)
        else:
            beta = rr / scal[g, 7 + k]
            alpha = rr / (rw - beta * rr / scal[g, k - 1])
        scal[g, k] = alpha
        scal[g, 4 + k] = beta
        return alpha, beta

    def up_copy(k, g):
        dst = hb.at[k, g, pl.ds(0, HALO)] if k < 2 else hb2.at[g]
        return pltpu.make_async_remote_copy(
            src_ref=w.at[k % 2, g, pl.ds(SX - HALO, HALO)],
            dst_ref=dst,
            send_sem=h_send.at[k, g, 0],
            recv_sem=h_recv.at[k, g, 0],
            device_id={"dom": d + 1},
        )

    def down_copy(k, g):
        dst = hb.at[k, g, pl.ds(HALO, HALO)] if k < 2 else hb2.at[g]
        return pltpu.make_async_remote_copy(
            src_ref=w.at[k % 2, g, pl.ds(0, HALO)],
            dst_ref=dst,
            send_sem=h_send.at[k, g, 1],
            recv_sem=h_recv.at[k, g, 1],
            device_id={"dom": d - 1},
        )

    def goes_up(k, g):
        return (d < N_DOM - 1) if k < 2 else ((d < N_DOM - 1) & (g == 0))

    def goes_down(k, g):
        return (d > 0) if k < 2 else ((d > 0) & (g == 1))

    def comes_up(k, g):
        return (d > 0) if k < 2 else ((d > 0) & (g == 0))

    def comes_down(k, g):
        return (d < N_DOM - 1) if k < 2 else ((d < N_DOM - 1) & (g == 1))

    def send_halo(k, g):
        @pl.when(goes_up(k, g))
        def _():
            up_copy(k, g).start()

        @pl.when(goes_down(k, g))
        def _():
            down_copy(k, g).start()

    def take_halo(k, g):
        @pl.when(comes_up(k, g))
        def _():
            up_copy(k, g).wait_recv()

        @pl.when(comes_down(k, g))
        def _():
            down_copy(k, g).wait_recv()

    def halo_sent(k, g):
        @pl.when(goes_up(k, g))
        def _():
            up_copy(k, g).wait_send()

        @pl.when(goes_down(k, g))
        def _():
            down_copy(k, g).wait_send()

    def stencil(g, x, y0, level):
        line = r[g, x + HALO, pl.ds(y0, 20)]
        f = line[HALO : HALO + 8]
        acc = (potb[pl.ds(x * NY + y0, 8)] + level[None]) * f
        for k in range(1, 7):
            pair = (
                line[HALO + k : HALO + k + 8]
                + line[HALO - k : HALO - k + 8]
                + r[g, x + HALO + k, pl.ds(y0 + HALO, 8)]
                + r[g, x + HALO - k, pl.ds(y0 + HALO, 8)]
            )
            acc = acc + (-0.5 * C[k]) * pair
        deep = jnp.dot(both_parts(f.reshape(64, NZ), 1), tz[...], preferred_element_type=F32)
        return f, acc + (deep[:, :NZ] + deep[:, NZ:]).reshape(8, 8, NZ)

    def tree(parts):
        parts = [parts[j] for j in range(8)]
        while len(parts) > 1:
            parts = [a + b for a, b in zip(parts[::2], parts[1::2])]
        return parts[0]

    none = jnp.zeros((8, NZ), F32)

    def level_of(g):
        return jnp.broadcast_to(lev[g], (8, NZ))

    def main(k, g):
        level = level_of(g)
        coeff = tot[g, 0] * energy[...]
        coeff = jnp.where(lanes < SLOTS, coeff, pltpu.roll(coeff, SLOTS, 1))
        lhs[...] = both_parts(coeff, 0)

        def body(i, carry):
            rr, rw, acc = carry
            x = i // 4
            y0 = pl.multiple_of((i % 4) * 8, 8)
            row = x * NY + y0
            f, image = stencil(g, x, y0, level)
            left = lhs[:, : 2 * SLOTS]
            blocks = []
            for j in range(8):
                v = jnp.dot(left, table[row + j], preferred_element_type=F32)
                blocks.append(image[j] + (v[:8] + v[8:]))
            for j in range(8):
                w[k % 2, g, x, y0 + j] = blocks[j]
            rr = rr + tree(f * f)
            rw = rw + tree([f[j] * blocks[j] for j in range(8)])
            return rr, rw, project(blocks, row, acc)

        rr, rw, acc = lax.fori_loop(
            0, SX * NY // 8, body, (none, none, jnp.zeros((16, 2 * SLOTS), F32))
        )
        send_sums(k, g, rr, rw)
        send_projections(k + 1, g, acc)
        send_halo(k, g)

    def last(g):
        level = level_of(g)

        def body(i, carry):
            rr, rw = carry
            x = i // 4
            y0 = pl.multiple_of((i % 4) * 8, 8)
            f, image = stencil(g, x, y0, level)
            return rr + tree(f * f), rw + tree(f * image)

        rr, rw = lax.fori_loop(0, SX * NY // 8, body, (none, none))
        own = (lanes >= ATOM_DEV) & (lanes < 2 * ATOM_DEV)
        t = tot[g, 0]
        rw = rw + jnp.where(own, t * t * energy[...], 0.0)
        send_sums(3, g, rr, rw)

    def update(k, g):
        alpha, beta = take_sums(k - 1, g)
        t = gathered_projections(k, g)
        if k > 1:
            t = t + beta * tot[g, 1]
        tot[g, 1] = t
        tot[g, 0] = tot[g, 0] - alpha * t
        a, b = alpha[None], beta[None]

        def own(i, _):
            x = i // 4
            y0 = pl.multiple_of((i % 4) * 8, 8)
            step = w[(k - 1) % 2, g, x, pl.ds(y0, 8)]
            if k > 1:
                step = step + b * s[g, x + HALO, pl.ds(y0, 8)]
            if k < 3:
                s[g, x + HALO, pl.ds(y0, 8)] = step
            new = r[g, x + HALO, pl.ds(y0 + HALO, 8)] - a * step
            r[g, x + HALO, pl.ds(y0 + HALO, 8)] = new
            if k < 3:
                hist[k, g, x, pl.ds(y0, 8)] = new
            return 0

        lax.fori_loop(0, SX * 4, own, 0)
        take_halo(k - 1, g)

        if k < 3:

            def side(i, _):
                x = i // 4
                y0 = pl.multiple_of((i % 4) * 8, 8)
                to = jnp.where(x < HALO, x, x + SX)
                step = hb[k - 1, g, x, pl.ds(y0, 8)]
                if k > 1:
                    step = step + b * s[g, to, pl.ds(y0, 8)]
                s[g, to, pl.ds(y0, 8)] = step
                r[g, to, pl.ds(y0 + HALO, 8)] = r[g, to, pl.ds(y0 + HALO, 8)] - a * step
                return 0

            lax.fori_loop(0, 2 * HALO * 4, side, 0)
        else:
            base = jnp.where(g == 0, 0, HALO + SX)
            other = HALO + SX - base

            def one_side(i, _):
                x = i // 4
                y0 = pl.multiple_of((i % 4) * 8, 8)
                step = hb2[g, x, pl.ds(y0, 8)] + b * s[g, base + x, pl.ds(y0, 8)]
                new = r[g, base + x, pl.ds(y0 + HALO, 8)] - a * step
                r[g, base + x, pl.ds(y0 + HALO, 8)] = new + new
                r[g, other + x, pl.ds(y0 + HALO, 8)] = jnp.zeros((8, 8, NZ), F32)
                return 0

            lax.fori_loop(0, HALO * 4, one_side, 0)

    loads[-1].wait()
    for g in range(2):
        for c in loads[4 * g : 4 * g + 4]:
            c.wait()

    def each(body):
        def run(g, _):
            body(g)
            return 0

        lax.fori_loop(0, 2, run, 0)

    def begin(g):
        def body(i, acc):
            x = i // 4
            y0 = pl.multiple_of((i % 4) * 8, 8)
            f = r[g, x + HALO, pl.ds(y0 + HALO, 8)]
            return project([f[j] for j in range(8)], x * NY + y0, acc)

        acc = lax.fori_loop(0, SX * NY // 8, body, jnp.zeros((16, 2 * SLOTS), F32))
        send_projections(0, g, acc)

    each(begin)

    def first(g):
        tot[g, 0] = gathered_projections(0, g)
        main(0, g)

    each(first)
    each(lambda g: forward_sums(0, g))

    for k in (1, 2):

        def turn(g, k=k):
            update(k, g)
            main(k, g)

        each(turn)
        each(lambda g, k=k: forward_sums(k, g))
        each(lambda g, k=k: halo_sent(k - 1, g))

    def closing(g):
        update(3, g)
        last(g)

    each(closing)
    each(lambda g: forward_sums(3, g))
    each(lambda g: halo_sent(2, g))

    def finish(g):
        a3, b3 = take_sums(3, g)
        g3 = a3
        g2 = scal[g, 2] + b3 * g3
        g1 = scal[g, 1] + scal[g, 6] * g2
        g0 = scal[g, 0] + scal[g, 5] * g1

        def body(i, _):
            x = i // 4
            y0 = pl.multiple_of((i % 4) * 8, 8)
            x_out[x, g, pl.ds(y0, 8)] = (
                g0[None] * hist[0, g, x, pl.ds(y0, 8)]
                + g1[None] * hist[1, g, x, pl.ds(y0, 8)]
                + g2[None] * hist[2, g, x, pl.ds(y0, 8)]
                + g3[None] * r[g, x + HALO, pl.ds(y0 + HALO, 8)]
            )
            return 0

        lax.fori_loop(0, SX * 4, body, 0)

    each(finish)


def solve(own, low, high, table, pot, lev, energy, tz):
    vmem = pl.BlockSpec(memory_space=pltpu.VMEM)
    anywhere = pl.BlockSpec(memory_space=pl.ANY)
    dma = pltpu.SemaphoreType.DMA
    return pl.pallas_call(
        solve_kernel,
        out_shape=jax.ShapeDtypeStruct((SX, 2, NY, 8, NZ), F32),
        in_specs=[anywhere] * 4 + [vmem] * 4,
        out_specs=vmem,
        scratch_shapes=[
            pltpu.VMEM((2, EXT, NYP, 8, NZ), F32),
            pltpu.VMEM((2, EXT, NY, 8, NZ), F32),
            pltpu.VMEM((2, 2, SX, NY, 8, NZ), F32),
            pltpu.VMEM((2, 2, 2 * HALO, NY, 8, NZ), F32),
            pltpu.VMEM((2, HALO, NY, 8, NZ), F32),
            pltpu.VMEM((3, 2, SX, NY, 8, NZ), F32),
            pltpu.VMEM((SX * NY, 2 * SLOTS, NZ), BF16),
            pltpu.VMEM((SX * NY, 8, NZ), F32),
            pltpu.VMEM((4, 2, PLANE, 8, NZ), F32),
            pltpu.VMEM((4, 2, DEPTH, 8, NZ), F32),
            pltpu.VMEM((4, 2, 4, 8, NZ), F32),
            pltpu.VMEM((4, 2, 2, 8, NZ), F32),
            pltpu.VMEM((4, 2, 8, NZ), F32),
            pltpu.VMEM((2, 12, 8, NZ), F32),
            pltpu.VMEM((2, 2, 8, NZ), F32),
            pltpu.VMEM((16, NZ), BF16),
            dma((9,)),
            dma((3, 2, 2)),
            dma((3, 2, 2)),
            dma((2, PLANE)),
            dma((2, 2, PLANE)),
            dma((2, DEPTH)),
            dma((2, 2, DEPTH)),
            dma((2, 4)),
            dma((2, 2, 4)),
        ],
        compiler_params=pltpu.CompilerParams(
            collective_id=0, has_side_effects=True, vmem_limit_bytes=60 * 2**20
        ),
        name="bicg_solve",
    )(own, low, high, table, pot, lev, energy, tz)


def cut_along(shard, dim, count):
    lengths = shard.shape
    tiles = shard.reshape(*lengths[:dim], count, lengths[dim] // count, *lengths[dim + 1 :])
    return jnp.moveaxis(tiles, dim, 0)


def summed_on_arrival(shard, axis, dim):
    count = lax.axis_size(axis)
    tiles = lax.all_to_all(cut_along(shard, dim, count), axis, 0, 0, tiled=True)
    return jnp.sum(tiles, axis=0)


def shards(orbitals, levels, potential, perturbation, projector, point_cell, point_atom, kb_energy):
    index = lax.axis_index("dom")
    up = [(i, i + 1) for i in range(N_DOM - 1)]
    down = [(i + 1, i) for i in range(N_DOM - 1)]
    right = -perturbation[None] * orbitals
    own = right.reshape(2, 8, SX, NY, NZ).transpose(2, 0, 3, 1, 4)
    low = lax.ppermute(own[SX - HALO :], "dom", up)
    high = lax.ppermute(own[:HALO], "dom", down)
    table = build_table(projector, point_cell, point_atom)
    energy = lax.dynamic_slice_in_dim(
        jnp.pad(kb_energy, (ATOM_DEV, ATOM_DEV)), index * ATOM_DEV, SLOTS
    )
    energy = jnp.pad(energy, (0, NZ - SLOTS))[None]
    lev = (-1.5 * C[0]) - levels.reshape(2, 8, 1)
    tz = jnp.asarray(depth_matrix())
    turned = solve(own, low, high, table, potential.reshape(SX * NY, NZ), lev, energy, tz)
    response = turned.transpose(1, 3, 0, 2, 4).reshape(orbitals.shape)
    density = summed_on_arrival(4.0 * jnp.sum(orbitals * response, axis=0), "st", 1)
    return response, density


def solution(mesh):
    in_specs = (
        P("st", "dom", None, None),
        P("st"),
        P("dom", None, None),
        P("dom", None, None),
        P("dom"),
        P("dom"),
        P("dom"),
        P(),
    )
    out_specs = (P("st", "dom", None, None), P("dom", "st", None))
    return jax.shard_map(shards, mesh=mesh, in_specs=in_specs, out_specs=out_specs, check_vma=False)
```

time: 784 us -> 209 us (0.27); the launches traced: 773 us -> 208 us
  other arithmetic: 369 us -> 3.9 us
  local copies, waits for them, and re-layouts: 190 us -> 12.7 us
  Pallas kernels: 0 us -> 175 us
  blocking collectives: 99.7 us -> 8.65 us
  starting transfers between devices: 59.2 us -> 7.02 us
  matrix products: 34 us -> 0 us
  waiting for transfers between devices: 19.7 us -> 0.01 us
    scatter-add x4 -> x0, other arithmetic: 245 us -> none  [operate(): jnp.zeros_like(flat).at[:, point_cell].add(spread).reshape(field.shape)]
    pallas_call x0 -> x2, Pallas kernels: none -> 175 us  [the longest x1 152 us: solve(): pl.pallas_call(solve_kernel, out_shape=jax.ShapeDtypeStruct((SX, 2, NY, 8...]
    reduce_sum x9 -> x1, other arithmetic: 109 us -> 0.51 us  [shards(): jnp.sum(orbitals * response, axis=0)]
    all_to_all x4 -> x0, blocking collectives: 91 us -> none  [sent_to_all(): lax.all_to_all(jnp.broadcast_to(shard[None], (count, *shard.shape)), axis...]
    gather x4 -> x0, local copies, waits for them, and re-layouts: 87.9 us -> none  [operate(): picked = flat[:, point_cell] * projector[None, :]]
    ppermute x24 -> x2, starting transfers between devices: 59.2 us -> 7.02 us  [the longest x1 5.1 us: shards(): high = lax.ppermute(own[:HALO], 'dom', down)]
    reshape x4 -> x1, local copies, waits for them, and re-layouts: 44.1 us -> 1.64 us  [shards(): own = right.reshape(2, 8, SX, NY, NZ).transpose(2, 0, 3, 1, 4)]
    dot_general x8 -> x0, matrix products: 34 us -> none  [the longest x4 31.5 us: operate(): partial_value = jnp.dot(picked, member, precision=HIGHEST)]
  transfers between devices with their start and end apart: 24 -> 2, of which waited for: 8 -> 0; matrix products, arithmetic and copies ran while one was open for 59% -> 1% of each run, Pallas kernels for 0% -> 11%
where the time goes in v1:
time: 209 us; the launch traced here: 208 us
  Pallas kernels  175 us (84%)
  local copies, waits for them, and re-layouts  12.7 us (6%)
  blocking collectives  8.65 us (4%)
  starting transfers between devices  7.02 us (3%)
  other arithmetic  3.9 us (2%)
    pallas_call x1, Pallas kernels, solve(): pl.pallas_call(solve_kernel, out_shape=jax.ShapeDtypeStruct((SX, 2, NY, 8...  152 us
    pallas_call x1, Pallas kernels, build_table(): pl.pallas_call(table_kernel, out_shape=jax.ShapeDtypeStruct((SX * NY, 2 *...  22.5 us
    all_to_all x1, blocking collectives, summed_on_arrival(): tiles = lax.all_to_all(cut_along(shard, dim, count), axis, 0, 0, tiled=True)  8.65 us
    unnamed x22, local copies, waits for them, and re-layouts  5.29 us
    ppermute x1, starting transfers between devices, shards(): high = lax.ppermute(own[:HALO], 'dom', down)  5.1 us
  transfers between devices with their start and end apart: 2, of which 0 were waited for; matrix products, arithmetic and copies ran while one was open for 1% of the time, Pallas kernels for 11%

profile of v1, /device:TPU:1, one launch (start us, length us, event | category | flops | bytes accessed | tf_op | source)
XLA Modules:
  0.0 207.6 jit_solution(4723620892418329365)
XLA Ops:
  0.6 0.9 neg.4
  1.5 1.8 broadcast_multiply_fusion
  3.4 1.6 copy.23
  5.0 0.0 copy-start.4
  5.1 0.0 copy-start.10
  5.1 0.0 copy-start.1
  5.1 0.0 copy-start.2
  5.1 0.0 copy-start.3
  5.1 2.3 %fusion = (f32[6,2,32,8,128]{4,3,2,1,0:T(8,128)}, f32[6,2,32,8,128]{4,3,2,1,0:T(8,128)}) fusion(f32[8,2,32,8,128]{4,3,2,1,0:T(8,128)S(1)} %bitcast.14), kind=kLoop, calls=%fused_computation.7 | loop fusion | bytes 6291456 | tf_op jit(solution)/shard_map/slice | solution.py:645
  7.4 0.0 copy-done.4
  7.4 5.1 %collective-permute-start.1 = (f32[6,2,32,8,128]{4,3,2,1,0:T(8,128)}, f32[6,2,32,8,128]{4,3,2,1,0:T(8,128)S(1)}, u32[]{:S(2)}, u32[]{:S(2)}) collective-permute-start(f32[6,2,32,8,128]{4,3,2,1,0:T(8,128)} %get-tuple-element.2), channel_id=1, source_target_pairs={{4,0},{8,4},{12,8},{16,12},{20,16},{24,20},{28,24},{32,28},{36,32}... | collective-permute-start | bytes 4718600 | tf_op jit(solution)/shard_map/ppermute | solution.py:645
  12.5 1.9 collective-permute-start
  14.4 0.0 copy-done.10
  14.4 0.7 sub.7.lev
  15.1 0.0 copy-done.1
  15.1 0.0 copy-done.2
  15.1 0.0 copy-done.3
  15.1 0.0 copy-start.9
  15.2 22.5 %projector_table.1.table_in = bf16[256,96,128]{2,1,0:T(8,128)(2,1)S(1)} custom-call(s32[8224]{0:T(1024)S(1)} %copy-done.1, s32[8224]{0:T(1024)S(1)} %copy-done.2, f32[8224]{0:T(1024)S(1)} %copy-done.3), custom_call_target="tpu_custom_call" | custom-call | bytes 41943040 | tf_op jit(solution)/shard_map/projector_table/pallas_call | solution.py:97
  37.7 0.0 copy-start
  37.7 2.7 %copy-done = bf16[256,96,128]{2,1,0:T(8,128)(2,1)} copy-done((bf16[256,96,128]{2,1,0:T(8,128)(2,1)}, bf16[256,96,128]{2,1,0:T(8,128)(2,1)S(1)}, u32[]{:S(2)}) %copy-start) | copy-done | bytes 6291480
  40.3 0.0 copy-done.9
  40.3 0.1 pad_dynamic-slice_fusion
  40.4 0.6 pad_bitcast_fusion.energy
  41.0 0.0 collective-permute-done.1.high_in
  41.0 0.0 copy-start.7
  41.0 0.0 collective-permute-done.low_in
  41.0 0.0 copy-start.8
  41.0 1.2 copy-done.7
  42.2 0.5 copy-done.8
  42.7 152.0 %bicg_solve.1 = f32[8,2,32,8,128]{4,3,2,1,0:T(8,128)} custom-call(f32[8,2,32,8,128]{4,3,2,1,0:T(8,128)} %bitcast.15, f32[6,2,32,8,128]{4,3,2,1,0:T(8,128)} %copy-done.8, f32[6,2,32,8,128]{4,3,2,1,0:T(8,128)} %copy-done.7, bf16[256,96,128]{2,1,0:T(8,128)(2,1)} %copy-done, f32[256,128]{1,0:T(8,128)} %bitcast.19, f32[2,8,1]{2,1,0:T(8,128)} %sub.7.lev, ...), custom_call_target="tpu_custom_call" | custom-call | tf_op jit(solution)/shard_map/bicg_solve/pallas_call | solution.py:587
  194.8 0.0 copy-start.5
  194.8 2.1 %copy.20 = f32[2,8,8,32,128]{4,3,2,1,0:T(8,128)S(1)} copy(f32[2,8,8,32,128]{4,1,3,0,2:T(8,128)} %bitcast.18) | data formatting | bytes 4194304 | tf_op jit(solution)/shard_map/transpose | solution.py:654
  196.9 0.1 copy-done.5
  197.0 0.0 copy-start.6
  197.0 0.5 multiply_reduce_fusion
  197.5 0.8 copy-done.6
  198.4 8.6 %all_to_all.5 = f32[4,8,8,128]{3,2,1,0:T(8,128)S(1)} all-to-all(f32[4,8,8,128]{3,2,1,0:T(8,128)S(1)} %copy.21), channel_id=1, replica_groups=mesh['dom'=64,'st'=4] {'st'}, dimensions={0} | all-to-all | bytes 262144 | tf_op jit(solution)/shard_map/all_to_all | solution.py:634
  207.0 0.6 reduce_sum.19
  (3 shorter events, 0.0 us)
Async XLA Ops:
  5.0 2.3 %copy-start.4 = (f32[2,8,8,32,128]{4,1,3,0,2:T(8,128)}, f32[2,8,8,32,128]{4,1,3,0,2:T(8,128)S(1)}, u32[]{:S(2)}) copy-start(f32[2,8,8,32,128]{4,1,3,0,2:T(8,128)S(1)} %copy.23) | copy-start | bytes 6291460
  5.1 9.4 %copy-start.10 = (f32[16]{0:T(128)S(1)}, f32[16]{0:T(128)}, u32[]{:S(2)}) copy-start(f32[16]{0:T(128)} %param.10) | copy-start | bytes 196
  5.1 10.1 %copy-start.1 = (s32[8224]{0:T(1024)S(1)}, s32[8224]{0:T(1024)}, u32[]{:S(2)}) copy-start(s32[8224]{0:T(1024)} %cell.1) | copy-start | bytes 98692
  5.1 10.1 %copy-start.2 = (s32[8224]{0:T(1024)S(1)}, s32[8224]{0:T(1024)}, u32[]{:S(2)}) copy-start(s32[8224]{0:T(1024)} %atom.1) | copy-start | bytes 98692
  5.1 10.1 %copy-start.3 = (f32[8224]{0:T(1024)S(1)}, f32[8224]{0:T(1024)}, u32[]{:S(2)}) copy-start(f32[8224]{0:T(1024)} %value.1) | copy-start | bytes 98692
  7.4 33.6 %collective-permute-start.1 = (f32[6,2,32,8,128]{4,3,2,1,0:T(8,128)}, f32[6,2,32,8,128]{4,3,2,1,0:T(8,128)S(1)}, u32[]{:S(2)}, u32[]{:S(2)}) collective-permute-start(f32[6,2,32,8,128]{4,3,2,1,0:T(8,128)} %get-tuple-element.2), channel_id=1, source_target_pairs={{4,0},{8,4},{12,8},{16,12},{20,16},{24,20},{28,24},{32,28},{36,32}... | collective-permute-start | bytes 4718600 | tf_op jit(solution)/shard_map/ppermute | solution.py:645
  12.5 28.5 %collective-permute-start = (f32[6,2,32,8,128]{4,3,2,1,0:T(8,128)}, f32[6,2,32,8,128]{4,3,2,1,0:T(8,128)S(1)}, u32[]{:S(2)}, u32[]{:S(2)}) collective-permute-start(f32[6,2,32,8,128]{4,3,2,1,0:T(8,128)} %get-tuple-element.3), channel_id=1, source_target_pairs={{0,4},{4,8},{8,12},{12,16},{16,20},{20,24},{24,28},{28,32},{32,36}... | collective-permute-start | bytes 4718600 | tf_op jit(solution)/shard_map/ppermute | solution.py:644
  15.1 25.2 %copy-start.9 = (f32[1024]{0:T(1024)S(1)}, f32[1024]{0:T(1024)}, u32[]{:S(2)}) copy-start(f32[1024]{0:T(1024)} %param.16) | copy-start | bytes 12292
  37.7 2.7 %copy-start = (bf16[256,96,128]{2,1,0:T(8,128)(2,1)}, bf16[256,96,128]{2,1,0:T(8,128)(2,1)S(1)}, u32[]{:S(2)}) copy-start(bf16[256,96,128]{2,1,0:T(8,128)(2,1)S(1)} %projector_table.1.table_in) | copy-start | bytes 18874372
  41.0 1.2 copy-start.7
  41.0 1.7 copy-start.8
  194.8 2.2 %copy-start.5 = (f32[16,8,32,128]{3,2,1,0:T(8,128)S(1)}, f32[16,8,32,128]{3,2,1,0:T(8,128)}, u32[]{:S(2)}) copy-start(f32[16,8,32,128]{3,2,1,0:T(8,128)} %param.9) | copy-start | bytes 6291460
  197.0 1.3 copy-start.6

commit v2 on v1

--- a/solution.py
+++ b/solution.py
@@ -27,6 +27,10 @@
 F32 = jnp.float32
 BF16 = jnp.bfloat16
 UNROLL = 8
+VMEM_MIB = 36
+ROWS = 32
+UNUSED = SX * NY * SLOTS * NZ
+SWAP = False
 
 
 def depth_matrix():
@@ -45,20 +49,19 @@
     return jnp.concatenate([high, value - high], axis=axis).astype(BF16)
 
 
-def table_kernel(cell, atom, value, table, dense):
-    first = (lax.axis_index("dom") - 1) * ATOM_DEV
-    slots = cell.shape[0]
+def table_kernel(place, value, table, dense):
+    slots = place.shape[0]
 
     def clear(i, _):
         dense[pl.ds(pl.multiple_of(i * 64, 64), 64), :] = jnp.zeros((64, NZ), F32)
         return 0
 
-    lax.fori_loop(0, dense.shape[0] // 64, clear, 0)
+    lax.fori_loop(0, SX * NY * SLOTS // 64, clear, 0)
 
     def halve(_, ends):
         low, high = ends
         mid = (low + high) // 2
-        used = atom[jnp.minimum(mid, slots - 1)] >= 0
+        used = place[jnp.minimum(mid, slots - 1)] < UNUSED
         go = low < high
         return (
             jnp.where(go & used, mid + 1, low),
@@ -70,47 +73,45 @@
 
     def put(i, _):
         for u in range(UNROLL):
-            s = i * UNROLL + u
-            c = cell[s]
-            a = atom[s] - first
-            live = s < used
-            row = jnp.where(live, (c >> 7) * SLOTS + a, 0)
-            lane = jnp.where(live, c & 127, -1)
+            where = place[i * UNROLL + u]
             pltpu.store(
-                dense.at[pl.ds(row, 1), :],
-                jnp.full((1, NZ), value[s], F32),
-                mask=lanes == lane,
+                dense.at[pl.ds(where >> 7, 1), :],
+                jnp.full((1, NZ), value[i * UNROLL + u], F32),
+                mask=lanes == (where & 127),
             )
         return 0
 
     lax.fori_loop(0, (used + UNROLL - 1) // UNROLL, put, 0)
 
     def split(i, _):
-        table[i] = both_parts(dense[pl.ds(pl.multiple_of(i * SLOTS, SLOTS), SLOTS), :], 0)
+        for j in range(4):
+            row = i * 4 + j
+            part = dense[pl.ds(pl.multiple_of(row * SLOTS, SLOTS), SLOTS), :]
+            table[row] = both_parts(part, 0)
         return 0
 
-    lax.fori_loop(0, SX * NY, split, 0)
-
-
-def build_table(projector, point_cell, point_atom):
+    lax.fori_loop(0, SX * NY // 4, split, 0)
+
+
+def build_table(projector, place):
     smem = pl.BlockSpec(memory_space=pltpu.SMEM)
     return pl.pallas_call(
         table_kernel,
         out_shape=jax.ShapeDtypeStruct((SX * NY, 2 * SLOTS, NZ), BF16),
-        in_specs=[smem, smem, smem],
+        in_specs=[smem, smem],
         out_specs=pl.BlockSpec(memory_space=pltpu.VMEM),
-        scratch_shapes=[pltpu.VMEM((SX * NY * SLOTS, NZ), F32)],
-        compiler_params=pltpu.CompilerParams(vmem_limit_bytes=40 * 2**20),
+        scratch_shapes=[pltpu.VMEM((SX * NY * SLOTS + 8, NZ), F32)],
+        compiler_params=pltpu.CompilerParams(vmem_limit_bytes=10 * 2**20),
         cost_estimate=pl.CostEstimate(flops=0, bytes_accessed=40 * 2**20, transcendentals=0),
         name="projector_table",
-    )(point_cell, point_atom, projector)
+    )(place, projector)
 
 
 def solve_kernel(
-    own_in, low_in, high_in, table_in, pot_in, lev, energy, tz,
-    x_out,
-    r, s, w, hb, hb2, hist, table, potb, st1, st2, pj, msg, pmsg, scal, tot, lhs,
-    sem_in, h_send, h_recv, a_send, a_recv, b_send, b_recv, p_send, p_recv,
+    own_in, low_in, high_in, table, orb, pot_in, lev, energy, tz,
+    x_out, dens_out,
+    r, s, w, hb, hb2, hist, potb, st1, st2, pj, msg, pmsg, scal, tot, lhs, dens, parts,
+    sem_in, h_send, h_recv, a_send, a_recv, b_send, b_recv, p_send, p_recv, d_send, d_recv,
 ):
     d = lax.axis_index("dom")
     zi = d // PLANE
@@ -120,12 +121,10 @@
     loads = []
     for g in range(2):
         loads += [
-            pltpu.make_async_copy(own_in.at[:, g], r.at[g, pl.ds(HALO, SX), inner], sem_in.at[4 * g]),
-            pltpu.make_async_copy(low_in.at[:, g], r.at[g, pl.ds(0, HALO), inner], sem_in.at[4 * g + 1]),
-            pltpu.make_async_copy(high_in.at[:, g], r.at[g, pl.ds(HALO + SX, HALO), inner], sem_in.at[4 * g + 2]),
-            pltpu.make_async_copy(own_in.at[:, g], hist.at[0, g], sem_in.at[4 * g + 3]),
+            pltpu.make_async_copy(own_in.at[:, g], r.at[g, pl.ds(HALO, SX), inner], sem_in.at[g, 0]),
+            pltpu.make_async_copy(low_in.at[:, g], r.at[g, pl.ds(0, HALO), inner], sem_in.at[g, 1]),
+            pltpu.make_async_copy(high_in.at[:, g], r.at[g, pl.ds(HALO + SX, HALO), inner], sem_in.at[g, 2]),
         ]
-    loads.append(pltpu.make_async_copy(table_in, table, sem_in.at[8]))
     for c in loads:
         c.start()
 
@@ -172,8 +171,16 @@
     def in_column(i):
         return ((zi + i) % DEPTH) * PLANE + ji
 
+    me = lax.axis_index("st")
+    blocks_st = lax.axis_size("st")
+
+    def other_block(i):
+        return (me + i) % blocks_st
+
     barrier = pltpu.get_barrier_semaphore()
-    count = jnp.int32(PLANE - 1 + DEPTH - 1)
+    count = jnp.int32(PLANE - 1 + DEPTH - 1 + blocks_st - 1)
+    for i in range(1, blocks_st):
+        pl.semaphore_signal(barrier, inc=1, device_id={"st": other_block(i)})
     for i in range(1, PLANE):
         pl.semaphore_signal(barrier, inc=1, device_id={"dom": in_plane(i)})
     for i in range(1, DEPTH):
@@ -199,6 +206,8 @@
     def project(blocks, row, acc):
         left = jnp.concatenate([both_parts(b, 0) for b in blocks], axis=1)
         right = jnp.concatenate([table[row + j] for j in range(len(blocks))], axis=1)
+        if SWAP:
+            left, right = right, left
         return acc + lax.dot_general(
             left, right, (((1,), (1,)), ((), ())), preferred_element_type=F32
         )
@@ -223,8 +232,14 @@
         )
 
     def send_projections(k, g, acc):
-        part = acc[:8, :SLOTS] + acc[8:, :SLOTS] + acc[:8, SLOTS:] + acc[8:, SLOTS:]
-        pmsg[k, g] = jnp.concatenate([part, jnp.zeros((8, NZ - SLOTS), F32)], axis=1)
+        if SWAP:
+            acc = acc[:SLOTS] + acc[SLOTS:]
+            acc = jnp.concatenate([acc, jnp.zeros((SLOTS, NZ - 16), F32)], axis=1)
+            acc = jnp.concatenate([acc, jnp.zeros((NZ - SLOTS, NZ), F32)], axis=0).T
+            pmsg[k, g] = acc[:8] + acc[8:16]
+        else:
+            part = acc[:8, :SLOTS] + acc[8:, :SLOTS] + acc[:8, SLOTS:] + acc[8:, SLOTS:]
+            pmsg[k, g] = jnp.concatenate([part, jnp.zeros((8, NZ - SLOTS), F32)], axis=1)
         for n in range(4):
 
             @pl.when(near[n][1])
@@ -381,20 +396,28 @@
         def _():
             down_copy(k, g).wait_send()
 
-    def stencil(g, x, y0, level):
-        line = r[g, x + HALO, pl.ds(y0, 20)]
-        f = line[HALO : HALO + 8]
-        acc = (potb[pl.ds(x * NY + y0, 8)] + level[None]) * f
-        for k in range(1, 7):
-            pair = (
-                line[HALO + k : HALO + k + 8]
-                + line[HALO - k : HALO - k + 8]
-                + r[g, x + HALO + k, pl.ds(y0 + HALO, 8)]
-                + r[g, x + HALO - k, pl.ds(y0 + HALO, 8)]
-            )
-            acc = acc + (-0.5 * C[k]) * pair
-        deep = jnp.dot(both_parts(f.reshape(64, NZ), 1), tz[...], preferred_element_type=F32)
-        return f, acc + (deep[:, :NZ] + deep[:, NZ:]).reshape(8, 8, NZ)
+    def stencil(g, x, y0, level, rows):
+        f = r[g, x + HALO, pl.ds(y0 + HALO, rows)]
+        deep = jnp.dot(
+            both_parts(f.reshape(rows * 8, NZ), 1), tz[...], preferred_element_type=F32
+        )
+        deep = (deep[:, :NZ] + deep[:, NZ:]).reshape(rows, 8, NZ)
+        fs, images = [], []
+        for part in range(0, rows, 8):
+            line = r[g, x + HALO, pl.ds(y0 + part, 20)]
+            f = line[HALO : HALO + 8]
+            acc = deep[part : part + 8] + (potb[pl.ds(x * NY + y0 + part, 8)] + level[None]) * f
+            for k in range(1, 7):
+                pair = (
+                    line[HALO + k : HALO + k + 8]
+                    + line[HALO - k : HALO - k + 8]
+                    + r[g, x + HALO + k, pl.ds(y0 + part + HALO, 8)]
+                    + r[g, x + HALO - k, pl.ds(y0 + part + HALO, 8)]
+                )
+                acc = acc + (-0.5 * C[k]) * pair
+            fs.append(f)
+            images.append(acc)
+        return fs, images
 
     def tree(parts):
         parts = [parts[j] for j in range(8)]
@@ -402,6 +425,10 @@
             parts = [a + b for a, b in zip(parts[::2], parts[1::2])]
         return parts[0]
 
+    def place(i):
+        per = NY // ROWS
+        return i // per, pl.multiple_of((i % per) * ROWS, ROWS)
+
     none = jnp.zeros((8, NZ), F32)
 
     def level_of(g):
@@ -415,23 +442,24 @@
 
         def body(i, carry):
             rr, rw, acc = carry
-            x = i // 4
-            y0 = pl.multiple_of((i % 4) * 8, 8)
-            row = x * NY + y0
-            f, image = stencil(g, x, y0, level)
+            x, y0 = place(i)
+            fs, images = stencil(g, x, y0, level, ROWS)
             left = lhs[:, : 2 * SLOTS]
-            blocks = []
-            for j in range(8):
-                v = jnp.dot(left, table[row + j], preferred_element_type=F32)
-                blocks.append(image[j] + (v[:8] + v[8:]))
-            for j in range(8):
-                w[k % 2, g, x, y0 + j] = blocks[j]
-            rr = rr + tree(f * f)
-            rw = rw + tree([f[j] * blocks[j] for j in range(8)])
-            return rr, rw, project(blocks, row, acc)
+            for n, (f, image) in enumerate(zip(fs, images)):
+                row = x * NY + y0 + n * 8
+                blocks = []
+                for j in range(8):
+                    v = jnp.dot(left, table[row + j], preferred_element_type=F32)
+                    blocks.append(image[j] + (v[:8] + v[8:]))
+                for j in range(8):
+                    w[k % 2, g, x, y0 + n * 8 + j] = blocks[j]
+                rr = rr + tree(f * f)
+                rw = rw + tree([f[j] * blocks[j] for j in range(8)])
+                acc = project(blocks, row, acc)
+            return rr, rw, acc
 
         rr, rw, acc = lax.fori_loop(
-            0, SX * NY // 8, body, (none, none, jnp.zeros((16, 2 * SLOTS), F32))
+            0, SX * NY // ROWS, body, (none, none, jnp.zeros((2 * SLOTS, 16) if SWAP else (16, 2 * SLOTS), F32))
         )
         send_sums(k, g, rr, rw)
         send_projections(k + 1, g, acc)
@@ -442,12 +470,12 @@
 
         def body(i, carry):
             rr, rw = carry
-            x = i // 4
-            y0 = pl.multiple_of((i % 4) * 8, 8)
-            f, image = stencil(g, x, y0, level)
-            return rr + tree(f * f), rw + tree(f * image)
-
-        rr, rw = lax.fori_loop(0, SX * NY // 8, body, (none, none))
+            x, y0 = place(i)
+            for f, image in zip(*stencil(g, x, y0, level, ROWS)):
+                rr, rw = rr + tree(f * f), rw + tree(f * image)
+            return rr, rw
+
+        rr, rw = lax.fori_loop(0, SX * NY // ROWS, body, (none, none))
         own = (lanes >= ATOM_DEV) & (lanes < 2 * ATOM_DEV)
         t = tot[g, 0]
         rw = rw + jnp.where(own, t * t * energy[...], 0.0)
@@ -473,7 +501,7 @@
             new = r[g, x + HALO, pl.ds(y0 + HALO, 8)] - a * step
             r[g, x + HALO, pl.ds(y0 + HALO, 8)] = new
             if k < 3:
-                hist[k, g, x, pl.ds(y0, 8)] = new
+                hist[k - 1, g, x, pl.ds(y0, 8)] = new
             return 0
 
         lax.fori_loop(0, SX * 4, own, 0)
@@ -508,11 +536,6 @@
 
             lax.fori_loop(0, HALO * 4, one_side, 0)
 
-    loads[-1].wait()
-    for g in range(2):
-        for c in loads[4 * g : 4 * g + 4]:
-            c.wait()
-
     def each(body):
         def run(g, _):
             body(g)
@@ -524,37 +547,47 @@
         def body(i, acc):
             x = i // 4
             y0 = pl.multiple_of((i % 4) * 8, 8)
-            f = r[g, x + HALO, pl.ds(y0 + HALO, 8)]
+            f = own_in[x, g, pl.ds(y0, 8)]
             return project([f[j] for j in range(8)], x * NY + y0, acc)
 
-        acc = lax.fori_loop(0, SX * NY // 8, body, jnp.zeros((16, 2 * SLOTS), F32))
+        acc = lax.fori_loop(0, SX * NY // 8, body, jnp.zeros((2 * SLOTS, 16) if SWAP else (16, 2 * SLOTS), F32))
         send_projections(0, g, acc)
 
     each(begin)
+    for c in loads:
+        c.wait()
+
+    def pass_on(k, g):
+        forward_sums(k - 1 + g, 1 - g)
 
     def first(g):
         tot[g, 0] = gathered_projections(0, g)
+
+        @pl.when(g == 1)
+        def _():
+            pass_on(0, g)
+
         main(0, g)
 
     each(first)
-    each(lambda g: forward_sums(0, g))
 
     for k in (1, 2):
 
         def turn(g, k=k):
             update(k, g)
+            pass_on(k, g)
             main(k, g)
 
         each(turn)
-        each(lambda g, k=k: forward_sums(k, g))
         each(lambda g, k=k: halo_sent(k - 1, g))
 
     def closing(g):
         update(3, g)
+        pass_on(3, g)
         last(g)
 
     each(closing)
-    each(lambda g: forward_sums(3, g))
+    forward_sums(3, 1)
     each(lambda g: halo_sent(2, g))
 
     def finish(g):
@@ -567,36 +600,69 @@
         def body(i, _):
             x = i // 4
             y0 = pl.multiple_of((i % 4) * 8, 8)
-            x_out[x, g, pl.ds(y0, 8)] = (
-                g0[None] * hist[0, g, x, pl.ds(y0, 8)]
-                + g1[None] * hist[1, g, x, pl.ds(y0, 8)]
-                + g2[None] * hist[2, g, x, pl.ds(y0, 8)]
+            value = (
+                g0[None] * own_in[x, g, pl.ds(y0, 8)]
+                + g1[None] * hist[0, g, x, pl.ds(y0, 8)]
+                + g2[None] * hist[1, g, x, pl.ds(y0, 8)]
                 + g3[None] * r[g, x + HALO, pl.ds(y0 + HALO, 8)]
             )
+            x_out[x, g, pl.ds(y0, 8)] = value
+            part = 4.0 * jnp.sum(value * orb[x, g, pl.ds(y0, 8)], axis=1)
+            dens[x, pl.ds(y0, 8), :] = jnp.where(g == 0, part, dens[x, pl.ds(y0, 8), :] + part)
             return 0
 
         lax.fori_loop(0, SX * 4, body, 0)
 
+    def clear_dens(i, _):
+        dens[i] = jnp.zeros((NY, NZ), F32)
+        return 0
+
+    lax.fori_loop(0, SX, clear_dens, 0)
     each(finish)
 
-
-def solve(own, low, high, table, pot, lev, energy, tz):
+    def rows_of(block):
+        return pl.ds(pl.multiple_of(block * (NY // blocks_st), NY // blocks_st), NY // blocks_st)
+
+    def block_copy(i, source):
+        return pltpu.make_async_remote_copy(
+            src_ref=dens.at[:, rows_of(other_block(i)), :],
+            dst_ref=parts.at[source],
+            send_sem=d_send.at[i],
+            recv_sem=d_recv.at[i],
+            device_id={"st": other_block(i)},
+        )
+
+    for i in range(1, blocks_st):
+        block_copy(i, me).start()
+    parts[me] = dens[:, rows_of(me), :]
+    for i in range(1, blocks_st):
+        block_copy(i, (me + blocks_st - i) % blocks_st).wait_recv()
+    total = parts[0]
+    for i in range(1, blocks_st):
+        total = total + parts[i]
+    dens_out[...] = total
+    for i in range(1, blocks_st):
+        block_copy(i, me).wait_send()
+
+
+def solve(own, low, high, table, orb, pot, lev, energy, tz, blocks_st):
     vmem = pl.BlockSpec(memory_space=pltpu.VMEM)
-    anywhere = pl.BlockSpec(memory_space=pl.ANY)
     dma = pltpu.SemaphoreType.DMA
     return pl.pallas_call(
         solve_kernel,
-        out_shape=jax.ShapeDtypeStruct((SX, 2, NY, 8, NZ), F32),
-        in_specs=[anywhere] * 4 + [vmem] * 4,
-        out_specs=vmem,
+        out_shape=(
+            jax.ShapeDtypeStruct((SX, 2, NY, 8, NZ), F32),
+            jax.ShapeDtypeStruct((SX, NY // blocks_st, NZ), F32),
+        ),
+        in_specs=[vmem] * 9,
+        out_specs=(vmem, vmem),
         scratch_shapes=[
             pltpu.VMEM((2, EXT, NYP, 8, NZ), F32),
             pltpu.VMEM((2, EXT, NY, 8, NZ), F32),
             pltpu.VMEM((2, 2, SX, NY, 8, NZ), F32),
             pltpu.VMEM((2, 2, 2 * HALO, NY, 8, NZ), F32),
             pltpu.VMEM((2, HALO, NY, 8, NZ), F32),
-            pltpu.VMEM((3, 2, SX, NY, 8, NZ), F32),
-            pltpu.VMEM((SX * NY, 2 * SLOTS, NZ), BF16),
+            pltpu.VMEM((2, 2, SX, NY, 8, NZ), F32),
             pltpu.VMEM((SX * NY, 8, NZ), F32),
             pltpu.VMEM((4, 2, PLANE, 8, NZ), F32),
             pltpu.VMEM((4, 2, DEPTH, 8, NZ), F32),
@@ -606,7 +672,9 @@
             pltpu.VMEM((2, 12, 8, NZ), F32),
             pltpu.VMEM((2, 2, 8, NZ), F32),
             pltpu.VMEM((16, NZ), BF16),
-            dma((9,)),
+            pltpu.VMEM((SX, NY, NZ), F32),
+            pltpu.VMEM((blocks_st, SX, NY // blocks_st, NZ), F32),
+            dma((2, 3)),
             dma((3, 2, 2)),
             dma((3, 2, 2)),
             dma((2, PLANE)),
@@ -615,44 +683,38 @@
             dma((2, 2, DEPTH)),
             dma((2, 4)),
             dma((2, 2, 4)),
+            dma((blocks_st,)),
+            dma((blocks_st,)),
         ],
         compiler_params=pltpu.CompilerParams(
-            collective_id=0, has_side_effects=True, vmem_limit_bytes=60 * 2**20
+            collective_id=0, has_side_effects=True, vmem_limit_bytes=VMEM_MIB * 2**20
         ),
         name="bicg_solve",
-    )(own, low, high, table, pot, lev, energy, tz)
-
-
-def cut_along(shard, dim, count):
-    lengths = shard.shape
-    tiles = shard.reshape(*lengths[:dim], count, lengths[dim] // count, *lengths[dim + 1 :])
-    return jnp.moveaxis(tiles, dim, 0)
-
-
-def summed_on_arrival(shard, axis, dim):
-    count = lax.axis_size(axis)
-    tiles = lax.all_to_all(cut_along(shard, dim, count), axis, 0, 0, tiled=True)
-    return jnp.sum(tiles, axis=0)
+    )(own, low, high, table, orb, pot, lev, energy, tz)
 
 
 def shards(orbitals, levels, potential, perturbation, projector, point_cell, point_atom, kb_energy):
     index = lax.axis_index("dom")
     up = [(i, i + 1) for i in range(N_DOM - 1)]
     down = [(i + 1, i) for i in range(N_DOM - 1)]
-    right = -perturbation[None] * orbitals
-    own = right.reshape(2, 8, SX, NY, NZ).transpose(2, 0, 3, 1, 4)
+    orb = orbitals.reshape(2, 8, SX, NY, NZ).transpose(2, 0, 3, 1, 4)
+    own = -(orb * perturbation[:, None, :, None, :])
     low = lax.ppermute(own[SX - HALO :], "dom", up)
     high = lax.ppermute(own[:HALO], "dom", down)
-    table = build_table(projector, point_cell, point_atom)
+    row = (point_cell >> 7) * SLOTS + point_atom - (index - 1) * ATOM_DEV
+    place = jnp.where(point_atom >= 0, row * NZ + (point_cell & 127), UNUSED)
+    table = build_table(projector, place)
     energy = lax.dynamic_slice_in_dim(
         jnp.pad(kb_energy, (ATOM_DEV, ATOM_DEV)), index * ATOM_DEV, SLOTS
     )
     energy = jnp.pad(energy, (0, NZ - SLOTS))[None]
     lev = (-1.5 * C[0]) - levels.reshape(2, 8, 1)
     tz = jnp.asarray(depth_matrix())
-    turned = solve(own, low, high, table, potential.reshape(SX * NY, NZ), lev, energy, tz)
+    turned, density = solve(
+        own, low, high, table, orb, potential.reshape(SX * NY, NZ), lev, energy, tz,
+        lax.axis_size("st"),
+    )
     response = turned.transpose(1, 3, 0, 2, 4).reshape(orbitals.shape)
-    density = summed_on_arrival(4.0 * jnp.sum(orbitals * response, axis=0), "st", 1)
     return response, density
 
 

time: 209 us -> 154 us (0.74)
  Pallas kernels: 175 us -> 132 us
  blocking collectives: 8.65 us -> 0 us
  local copies, waits for them, and re-layouts: 12.7 us -> 7.61 us
    pallas_call x1, Pallas kernels: 152 us -> 119 us  [solve(): pl.pallas_call(solve_kernel, out_shape=(jax.ShapeDtypeStruct((SX, 2, NY,...]
    pallas_call x1, Pallas kernels: 22.5 us -> 12.5 us  [build_table(): pl.pallas_call(table_kernel, out_shape=jax.ShapeDtypeStruct((SX * NY, 2 *...]
    all_to_all x1 -> x0, blocking collectives: 8.65 us -> none  [summed_on_arrival(): tiles = lax.all_to_all(cut_along(shard, dim, count), axis, 0, 0, tiled=True)]
    unnamed x22 -> x19, local copies, waits for them, and re-layouts: 5.29 us -> 0.67 us
    neg x1, other arithmetic: 0.92 us -> 3.53 us  [shards(): own = -(orb * perturbation[:, None, :, None, :])]
  transfers between devices with their start and end apart: 2 -> 2, of which waited for: 0 -> 2; matrix products, arithmetic and copies ran while one was open for 1% -> 2% of each run, Pallas kernels for 11% -> 8%
where the time goes in v2:
time: 154 us; the launch traced here: 153 us
  Pallas kernels  132 us (86%)
  local copies, waits for them, and re-layouts  7.61 us (5%)
  starting transfers between devices  7.02 us (5%)
  other arithmetic  3.55 us (2%)
  waiting for transfers between devices  1.81 us (1%)
    pallas_call x1, Pallas kernels, solve(): pl.pallas_call(solve_kernel, out_shape=(jax.ShapeDtypeStruct((SX, 2, NY,...  119 us
    pallas_call x1, Pallas kernels, build_table(): pl.pallas_call(table_kernel, out_shape=jax.ShapeDtypeStruct((SX * NY, 2 *...  12.5 us
    ppermute x1, starting transfers between devices, shards(): high = lax.ppermute(own[:HALO], 'dom', down)  5.1 us
    neg x1, other arithmetic, shards(): own = -(orb * perturbation[:, None, :, None, :])  3.53 us
  transfers between devices with their start and end apart: 2, of which 2 were waited for; matrix products, arithmetic and copies ran while one was open for 2% of the time, Pallas kernels for 8%

profile of v2, /device:TPU:1, one launch (start us, length us, event | category | flops | bytes accessed | tf_op | source)
XLA Modules:
  0.0 152.6 jit_solution(1882843861946858452)
XLA Ops:
  0.6 3.5 %multiply_negate_fusion.own_in = f32[8,2,32,8,128]{4,3,2,1,0:T(8,128)S(1)} fusion(f32[8,32,128]{2,1,0:T(8,128)} %param.12, f32[2,8,8,32,128]{4,3,2,1,0:T(8,128)} %bitcast.14), kind=kLoop, calls=%fused_computation.1 | loop fusion | flops 1048576 | bytes 4325376 | tf_op jit(solution)/shard_map/neg | solution.py:701
  4.2 0.0 copy-start.4
  4.2 2.1 %fusion = (f32[6,2,32,8,128]{4,3,2,1,0:T(8,128)}, f32[6,2,32,8,128]{4,3,2,1,0:T(8,128)}) fusion(f32[8,2,32,8,128]{4,3,2,1,0:T(8,128)S(1)} %multiply_negate_fusion.own_in), kind=kLoop, calls=%fused_computation.6 | loop fusion | bytes 6291456 | tf_op jit(solution)/shard_map/slice | solution.py:703
  6.3 5.1 %collective-permute-start.1 = (f32[6,2,32,8,128]{4,3,2,1,0:T(8,128)}, f32[6,2,32,8,128]{4,3,2,1,0:T(8,128)}, u32[]{:S(2)}, u32[]{:S(2)}) collective-permute-start(f32[6,2,32,8,128]{4,3,2,1,0:T(8,128)} %get-tuple-element.6), channel_id=1, source_target_pairs={{4,0},{8,4},{12,8},{16,12},{20,16},{24,20},{28,24},{32,28},{36,32}... | collective-permute-start | bytes 4718600 | tf_op jit(solution)/shard_map/ppermute | solution.py:703
  11.4 1.9 %collective-permute-start = (f32[6,2,32,8,128]{4,3,2,1,0:T(8,128)}, f32[6,2,32,8,128]{4,3,2,1,0:T(8,128)}, u32[]{:S(2)}, u32[]{:S(2)}) collective-permute-start(f32[6,2,32,8,128]{4,3,2,1,0:T(8,128)} %get-tuple-element.7), channel_id=1, source_target_pairs={{0,4},{4,8},{8,12},{12,16},{16,20},{20,24},{24,28},{28,32},{32,36}... | collective-permute-start | bytes 4718600 | tf_op jit(solution)/shard_map/ppermute | solution.py:702
  13.3 0.0 copy-done.4
  13.3 0.0 copy-start.8
  13.3 0.0 copy-start.5
  13.3 0.0 copy-start.6
  13.3 0.0 copy-start.3
  13.4 3.0 %copy.18 = f32[2,8,8,32,128]{4,1,3,0,2:T(8,128)} copy(f32[2,8,8,32,128]{4,3,2,1,0:T(8,128)S(1)} %bitcast.15) | data formatting | bytes 4194304 | tf_op jit(solution)/shard_map/reshape | solution.py:700
  16.3 0.0 copy-done.8
  16.3 0.1 sub.19.lev
  16.4 0.0 copy-done.5
  16.4 0.0 copy-done.6
  16.4 0.0 copy-done.3
  16.5 0.0 copy-start.7
  16.5 0.0 copy-start
  16.5 0.0 copy-start.1
  16.5 0.0 copy-start.2
  16.5 12.5 %projector_table.1.table = bf16[256,96,128]{2,1,0:T(8,128)(2,1)S(1)} custom-call(s32[8224]{0:T(1024)S(1)} %add_select_fusion.place, f32[8224]{0:T(1024)S(1)} %copy-done.3), custom_call_target="tpu_custom_call" | custom-call | bytes 41943040 | tf_op jit(solution)/shard_map/projector_table/pallas_call | solution.py:98
  29.0 0.0 copy-done.7
  29.0 0.1 pad_dynamic-slice_fusion
  29.1 0.1 collective-permute-done.1.high_in
  29.2 1.7 %collective-permute-done.low_in = f32[6,2,32,8,128]{4,3,2,1,0:T(8,128)} collective-permute-done((f32[6,2,32,8,128]{4,3,2,1,0:T(8,128)}, f32[6,2,32,8,128]{4,3,2,1,0:T(8,128)}, u32[]{:S(2)}, u32[]{:S(2)}) %collective-permute-start) | collective-permute-done | bytes 1572896 | tf_op jit(solution)/shard_map/ppermute | solution.py:702
  30.9 0.0 copy-done
  30.9 0.0 copy-done.1
  30.9 0.0 copy-done.2
  31.0 119.3 %bicg_solve.1 = (f32[8,2,32,8,128]{4,3,2,1,0:T(8,128)S(1)}, f32[8,8,128]{2,1,0:T(8,128)S(1)}) custom-call(f32[8,2,32,8,128]{4,3,2,1,0:T(8,128)S(1)} %multiply_negate_fusion.own_in, f32[6,2,32,8,128]{4,3,2,1,0:T(8,128)} %collective-permute-done.low_in, f32[6,2,32,8,128]{4,3,2,1,0:T(8,128)} %collective-permute-done.1.high_in, ...), custom_call_target="tpu_custom_call" | custom-call | tf_op jit(solution)/shard_map/bicg_solve/pallas_call | solution.py:651
  150.3 1.7 %copy.14 = f32[2,8,8,32,128]{4,3,2,1,0:T(8,128)} copy(f32[2,8,8,32,128]{4,1,3,0,2:T(8,128)S(1)} %bitcast.12) | data formatting | bytes 4194304 | tf_op jit(solution)/shard_map/transpose | solution.py:717
  152.0 0.6 copy.20
  (3 shorter events, 0.0 us)
Async XLA Ops:
  4.2 9.1 %copy-start.4 = (f32[16,8,32,128]{3,2,1,0:T(8,128)S(1)}, f32[16,8,32,128]{3,2,1,0:T(8,128)}, u32[]{:S(2)}) copy-start(f32[16,8,32,128]{3,2,1,0:T(8,128)} %param.9) | copy-start | bytes 6291460
  6.3 23.0 %collective-permute-start.1 = (f32[6,2,32,8,128]{4,3,2,1,0:T(8,128)}, f32[6,2,32,8,128]{4,3,2,1,0:T(8,128)}, u32[]{:S(2)}, u32[]{:S(2)}) collective-permute-start(f32[6,2,32,8,128]{4,3,2,1,0:T(8,128)} %get-tuple-element.6), channel_id=1, source_target_pairs={{4,0},{8,4},{12,8},{16,12},{20,16},{24,20},{28,24},{32,28},{36,32}... | collective-permute-start | bytes 4718600 | tf_op jit(solution)/shard_map/ppermute | solution.py:703
  11.4 19.6 %collective-permute-start = (f32[6,2,32,8,128]{4,3,2,1,0:T(8,128)}, f32[6,2,32,8,128]{4,3,2,1,0:T(8,128)}, u32[]{:S(2)}, u32[]{:S(2)}) collective-permute-start(f32[6,2,32,8,128]{4,3,2,1,0:T(8,128)} %get-tuple-element.7), channel_id=1, source_target_pairs={{0,4},{4,8},{8,12},{12,16},{16,20},{20,24},{24,28},{28,32},{32,36}... | collective-permute-start | bytes 4718600 | tf_op jit(solution)/shard_map/ppermute | solution.py:702
  13.3 3.0 %copy-start.8 = (f32[16]{0:T(128)S(1)}, f32[16]{0:T(128)}, u32[]{:S(2)}) copy-start(f32[16]{0:T(128)} %param.10) | copy-start | bytes 196
  13.3 3.1 %copy-start.5 = (s32[8224]{0:T(1024)S(1)}, s32[8224]{0:T(1024)}, u32[]{:S(2)}) copy-start(s32[8224]{0:T(1024)} %param.14) | copy-start | bytes 98692
  13.3 3.1 %copy-start.6 = (s32[8224]{0:T(1024)S(1)}, s32[8224]{0:T(1024)}, u32[]{:S(2)}) copy-start(s32[8224]{0:T(1024)} %param.15) | copy-start | bytes 98692
  13.3 3.1 %copy-start.3 = (f32[8224]{0:T(1024)S(1)}, f32[8224]{0:T(1024)}, u32[]{:S(2)}) copy-start(f32[8224]{0:T(1024)} %value.1) | copy-start | bytes 98692
  16.5 12.6 %copy-start.7 = (f32[1024]{0:T(1024)S(1)}, f32[1024]{0:T(1024)}, u32[]{:S(2)}) copy-start(f32[1024]{0:T(1024)} %param.16) | copy-start | bytes 12292
  16.5 14.5 %copy-start = (f32[2,8,8,32,128]{4,1,3,0,2:T(8,128)S(1)}, f32[2,8,8,32,128]{4,1,3,0,2:T(8,128)}, u32[]{:S(2)}) copy-start(f32[2,8,8,32,128]{4,1,3,0,2:T(8,128)} %copy.18) | copy-start | bytes 6291460
  16.5 14.5 %copy-start.1 = (f32[8,32,128]{2,1,0:T(8,128)S(1)}, f32[8,32,128]{2,1,0:T(8,128)}, u32[]{:S(2)}) copy-start(f32[8,32,128]{2,1,0:T(8,128)} %param.11) | copy-start | bytes 393220
  16.5 14.5 %copy-start.2 = (bf16[256,256]{1,0:T(8,128)(2,1)S(1)}, bf16[256,256]{1,0:T(8,128)(2,1)}, u32[]{:S(2)}) copy-start(bf16[256,256]{1,0:T(8,128)(2,1)} %constant.32.clone.tz) | copy-start | bytes 393220

commit v3 on v2

--- a/solution.py
+++ b/solution.py
@@ -27,10 +27,10 @@
 F32 = jnp.float32
 BF16 = jnp.bfloat16
 UNROLL = 8
-VMEM_MIB = 36
+VMEM_MIB = 43
 ROWS = 32
+BREAK = 2
 UNUSED = SX * NY * SLOTS * NZ
-SWAP = False
 
 
 def depth_matrix():
@@ -108,26 +108,16 @@
 
 
 def solve_kernel(
-    own_in, low_in, high_in, table, orb, pot_in, lev, energy, tz,
+    table, orb, pot_in, pert_in, lev, energy, tz,
     x_out, dens_out,
-    r, s, w, hb, hb2, hist, potb, st1, st2, pj, msg, pmsg, scal, tot, lhs, dens, parts,
-    sem_in, h_send, h_recv, a_send, a_recv, b_send, b_recv, p_send, p_recv, d_send, d_recv,
+    own_in, turned, r, s, w, hb, hb2, hist, potb, st1, st2, pj, msg, pmsg, scal, tot, lhs, dens, parts,
+    h_send, h_recv, a_send, a_recv, b_send, b_recv, p_send, p_recv, d_send, d_recv,
 ):
     d = lax.axis_index("dom")
     zi = d // PLANE
     ji = d % PLANE
     inner = pl.ds(HALO, NY)
 
-    loads = []
-    for g in range(2):
-        loads += [
-            pltpu.make_async_copy(own_in.at[:, g], r.at[g, pl.ds(HALO, SX), inner], sem_in.at[g, 0]),
-            pltpu.make_async_copy(low_in.at[:, g], r.at[g, pl.ds(0, HALO), inner], sem_in.at[g, 1]),
-            pltpu.make_async_copy(high_in.at[:, g], r.at[g, pl.ds(HALO + SX, HALO), inner], sem_in.at[g, 2]),
-        ]
-    for c in loads:
-        c.start()
-
     zero = jnp.zeros((HALO, 8, NZ), F32)
 
     def clear(i, _):
@@ -138,8 +128,23 @@
 
     lax.fori_loop(0, EXT, clear, 0)
 
+    def start(i, _):
+        x = i // 4
+        y0 = pl.multiple_of((i % 4) * 8, 8)
+        rows = pert_in[pl.ds(pl.multiple_of(i * 8, 8), 8), :]
+        for j in range(8):
+            row = jnp.broadcast_to(rows[j : j + 1, :], (8, NZ))
+            for g in range(2):
+                value = -row * orb[x, g, y0 + j]
+                own_in[x, g, y0 + j] = value
+                r[g, x + HALO, y0 + HALO + j] = value
+        return 0
+
+    lax.fori_loop(0, SX * NY // 8, start, 0)
+
     def clear_halo(base):
         plane = jnp.zeros((NY, 8, NZ), F32)
+        far = jnp.where(base == 0, 0, SX + HALO)
 
         def one(i, _):
             for k in range(2):
@@ -147,6 +152,7 @@
                     hb[k, g, base + i] = plane
             for g in range(2):
                 hb2[g, i] = plane
+                r[g, far + i, inner] = plane
             return 0
 
         lax.fori_loop(0, HALO, one, 0)
@@ -194,23 +200,12 @@
 
     lanes = lax.broadcasted_iota(jnp.int32, (8, NZ), 1)
 
-    def spread(i, _):
-        rows = pot_in[pl.ds(pl.multiple_of(i * 8, 8), 8), :]
-        for j in range(8):
-            potb[i * 8 + j] = jnp.broadcast_to(rows[j : j + 1, :], (8, NZ))
-        return 0
-
-    lax.fori_loop(0, SX * NY // 8, spread, 0)
     pl.semaphore_wait(barrier, count)
 
     def project(blocks, row, acc):
         left = jnp.concatenate([both_parts(b, 0) for b in blocks], axis=1)
-        right = jnp.concatenate([table[row + j] for j in range(len(blocks))], axis=1)
-        if SWAP:
-            left, right = right, left
-        return acc + lax.dot_general(
-            left, right, (((1,), (1,)), ((), ())), preferred_element_type=F32
-        )
+        right = turned[pl.ds(pl.multiple_of(row * NZ, 8 * NZ), 8 * NZ), :]
+        return acc + jnp.dot(left, right, preferred_element_type=F32)
 
     def near_copy(k, g, n):
         step = near[n][0]
@@ -232,14 +227,8 @@
         )
 
     def send_projections(k, g, acc):
-        if SWAP:
-            acc = acc[:SLOTS] + acc[SLOTS:]
-            acc = jnp.concatenate([acc, jnp.zeros((SLOTS, NZ - 16), F32)], axis=1)
-            acc = jnp.concatenate([acc, jnp.zeros((NZ - SLOTS, NZ), F32)], axis=0).T
-            pmsg[k, g] = acc[:8] + acc[8:16]
-        else:
-            part = acc[:8, :SLOTS] + acc[8:, :SLOTS] + acc[:8, SLOTS:] + acc[8:, SLOTS:]
-            pmsg[k, g] = jnp.concatenate([part, jnp.zeros((8, NZ - SLOTS), F32)], axis=1)
+        part = acc[:8, :SLOTS] + acc[8:, :SLOTS] + acc[:8, SLOTS:] + acc[8:, SLOTS:]
+        pmsg[k, g] = jnp.concatenate([part, jnp.zeros((8, NZ - SLOTS), F32)], axis=1)
         for n in range(4):
 
             @pl.when(near[n][1])
@@ -396,6 +385,51 @@
         def _():
             down_copy(k, g).wait_send()
 
+    def first_up(g):
+        return pltpu.make_async_remote_copy(
+            src_ref=own_in.at[pl.ds(SX - HALO, HALO), g],
+            dst_ref=r.at[g, pl.ds(0, HALO), inner],
+            send_sem=h_send.at[3, g, 0],
+            recv_sem=h_recv.at[3, g, 0],
+            device_id={"dom": d + 1},
+        )
+
+    def first_down(g):
+        return pltpu.make_async_remote_copy(
+            src_ref=own_in.at[pl.ds(0, HALO), g],
+            dst_ref=r.at[g, pl.ds(SX + HALO, HALO), inner],
+            send_sem=h_send.at[3, g, 1],
+            recv_sem=h_recv.at[3, g, 1],
+            device_id={"dom": d - 1},
+        )
+
+    def send_first(g):
+        @pl.when(d < N_DOM - 1)
+        def _():
+            first_up(g).start()
+
+        @pl.when(d > 0)
+        def _():
+            first_down(g).start()
+
+    def take_first(g):
+        @pl.when(d > 0)
+        def _():
+            first_up(g).wait_recv()
+
+        @pl.when(d < N_DOM - 1)
+        def _():
+            first_down(g).wait_recv()
+
+    def first_sent(g):
+        @pl.when(d < N_DOM - 1)
+        def _():
+            first_up(g).wait_send()
+
+        @pl.when(d > 0)
+        def _():
+            first_down(g).wait_send()
+
     def stencil(g, x, y0, level, rows):
         f = r[g, x + HALO, pl.ds(y0 + HALO, rows)]
         deep = jnp.dot(
@@ -434,7 +468,7 @@
     def level_of(g):
         return jnp.broadcast_to(lev[g], (8, NZ))
 
-    def main(k, g):
+    def main(k, g, between):
         level = level_of(g)
         coeff = tot[g, 0] * energy[...]
         coeff = jnp.where(lanes < SLOTS, coeff, pltpu.roll(coeff, SLOTS, 1))
@@ -442,6 +476,7 @@
 
         def body(i, carry):
             rr, rw, acc = carry
+            pl.when(i == BREAK)(between)
             x, y0 = place(i)
             fs, images = stencil(g, x, y0, level, ROWS)
             left = lhs[:, : 2 * SLOTS]
@@ -459,7 +494,7 @@
             return rr, rw, acc
 
         rr, rw, acc = lax.fori_loop(
-            0, SX * NY // ROWS, body, (none, none, jnp.zeros((2 * SLOTS, 16) if SWAP else (16, 2 * SLOTS), F32))
+            0, SX * NY // ROWS, body, (none, none, jnp.zeros((16, 2 * SLOTS), F32))
         )
         send_sums(k, g, rr, rw)
         send_projections(k + 1, g, acc)
@@ -543,31 +578,52 @@
 
         lax.fori_loop(0, 2, run, 0)
 
-    def begin(g):
-        def body(i, acc):
-            x = i // 4
-            y0 = pl.multiple_of((i % 4) * 8, 8)
-            f = own_in[x, g, pl.ds(y0, 8)]
-            return project([f[j] for j in range(8)], x * NY + y0, acc)
-
-        acc = lax.fori_loop(0, SX * NY // 8, body, jnp.zeros((2 * SLOTS, 16) if SWAP else (16, 2 * SLOTS), F32))
-        send_projections(0, g, acc)
-
-    each(begin)
-    for c in loads:
-        c.wait()
+    def begin(i, acc):
+        x = i // 4
+        y0 = pl.multiple_of((i % 4) * 8, 8)
+        row = pl.multiple_of(i * 8, 8)
+        left = []
+        for j in range(8):
+            left.append(
+                jnp.concatenate([both_parts(own_in[x, g, y0 + j], 0) for g in range(2)], axis=0)
+            )
+        right = []
+        for j in range(8):
+            right.append(table[row + j].astype(F32).T.astype(BF16))
+            turned[pl.ds(pl.multiple_of((row + j) * NZ, NZ), NZ), :] = right[-1]
+        return acc + jnp.dot(
+            jnp.concatenate(left, axis=1),
+            jnp.concatenate(right, axis=0),
+            preferred_element_type=F32,
+        )
+
+    send_first(0)
+    acc = lax.fori_loop(0, SX * NY // 8, begin, jnp.zeros((32, 2 * SLOTS), F32))
+    send_projections(0, 0, acc[:16])
+    send_projections(0, 1, acc[16:])
+    send_first(1)
+
+    def spread(i, _):
+        rows = pot_in[pl.ds(pl.multiple_of(i * 8, 8), 8), :]
+        for j in range(8):
+            potb[i * 8 + j] = jnp.broadcast_to(rows[j : j + 1, :], (8, NZ))
+        return 0
+
+    lax.fori_loop(0, SX * NY // 8, spread, 0)
 
     def pass_on(k, g):
         forward_sums(k - 1 + g, 1 - g)
 
     def first(g):
+        take_first(g)
         tot[g, 0] = gathered_projections(0, g)
 
-        @pl.when(g == 1)
-        def _():
-            pass_on(0, g)
-
-        main(0, g)
+        def between():
+            @pl.when(g == 1)
+            def _():
+                pass_on(0, g)
+
+        main(0, g, between)
 
     each(first)
 
@@ -575,11 +631,12 @@
 
         def turn(g, k=k):
             update(k, g)
-            pass_on(k, g)
-            main(k, g)
+            main(k, g, lambda: pass_on(k, g))
 
         each(turn)
         each(lambda g, k=k: halo_sent(k - 1, g))
+
+    each(first_sent)
 
     def closing(g):
         update(3, g)
@@ -645,7 +702,7 @@
         block_copy(i, me).wait_send()
 
 
-def solve(own, low, high, table, orb, pot, lev, energy, tz, blocks_st):
+def solve(table, orb, pot, pert, lev, energy, tz, blocks_st):
     vmem = pl.BlockSpec(memory_space=pltpu.VMEM)
     dma = pltpu.SemaphoreType.DMA
     return pl.pallas_call(
@@ -654,9 +711,11 @@
             jax.ShapeDtypeStruct((SX, 2, NY, 8, NZ), F32),
             jax.ShapeDtypeStruct((SX, NY // blocks_st, NZ), F32),
         ),
-        in_specs=[vmem] * 9,
+        in_specs=[vmem] * 7,
         out_specs=(vmem, vmem),
         scratch_shapes=[
+            pltpu.VMEM((SX, 2, NY, 8, NZ), F32),
+            pltpu.VMEM((SX * NY * NZ, 2 * SLOTS), BF16),
             pltpu.VMEM((2, EXT, NYP, 8, NZ), F32),
             pltpu.VMEM((2, EXT, NY, 8, NZ), F32),
             pltpu.VMEM((2, 2, SX, NY, 8, NZ), F32),
@@ -674,9 +733,8 @@
             pltpu.VMEM((16, NZ), BF16),
             pltpu.VMEM((SX, NY, NZ), F32),
             pltpu.VMEM((blocks_st, SX, NY // blocks_st, NZ), F32),
-            dma((2, 3)),
-            dma((3, 2, 2)),
-            dma((3, 2, 2)),
+            dma((4, 2, 2)),
+            dma((4, 2, 2)),
             dma((2, PLANE)),
             dma((2, 2, PLANE)),
             dma((2, DEPTH)),
@@ -690,17 +748,12 @@
             collective_id=0, has_side_effects=True, vmem_limit_bytes=VMEM_MIB * 2**20
         ),
         name="bicg_solve",
-    )(own, low, high, table, orb, pot, lev, energy, tz)
+    )(table, orb, pot, pert, lev, energy, tz)
 
 
 def shards(orbitals, levels, potential, perturbation, projector, point_cell, point_atom, kb_energy):
     index = lax.axis_index("dom")
-    up = [(i, i + 1) for i in range(N_DOM - 1)]
-    down = [(i + 1, i) for i in range(N_DOM - 1)]
     orb = orbitals.reshape(2, 8, SX, NY, NZ).transpose(2, 0, 3, 1, 4)
-    own = -(orb * perturbation[:, None, :, None, :])
-    low = lax.ppermute(own[SX - HALO :], "dom", up)
-    high = lax.ppermute(own[:HALO], "dom", down)
     row = (point_cell >> 7) * SLOTS + point_atom - (index - 1) * ATOM_DEV
     place = jnp.where(point_atom >= 0, row * NZ + (point_cell & 127), UNUSED)
     table = build_table(projector, place)
@@ -711,7 +764,7 @@
     lev = (-1.5 * C[0]) - levels.reshape(2, 8, 1)
     tz = jnp.asarray(depth_matrix())
     turned, density = solve(
-        own, low, high, table, orb, potential.reshape(SX * NY, NZ), lev, energy, tz,
+        table, orb, potential.reshape(SX * NY, NZ), perturbation.reshape(SX * NY, NZ), lev, energy, tz,
         lax.axis_size("st"),
     )
     response = turned.transpose(1, 3, 0, 2, 4).reshape(orbitals.shape)

time: 154 us -> 139 us (0.903)
  starting transfers between devices: 7.02 us -> 0 us
  Pallas kernels: 132 us -> 128 us
  other arithmetic: 3.55 us -> 1.47 us
  waiting for transfers between devices: 1.81 us -> 0 us
    ppermute x2 -> x0, starting transfers between devices: 7.02 us -> none  [the longest x1 5.1 us: shards(): high = lax.ppermute(own[:HALO], 'dom', down)]
    neg x1 -> x0, other arithmetic: 3.53 us -> none  [shards(): own = -(orb * perturbation[:, None, :, None, :])]
    pallas_call x1, Pallas kernels: 119 us -> 116 us  [solve(): pl.pallas_call(solve_kernel, out_shape=(jax.ShapeDtypeStruct((SX, 2, NY,...]
    slice x1 -> x0, local copies, waits for them, and re-layouts: 2.08 us -> none  [shards(): high = lax.ppermute(own[:HALO], 'dom', down)]
    ppermute x2 -> x0, waiting for transfers between devices: 1.81 us -> none  [the longest x1 1.71 us: shards(): low = lax.ppermute(own[SX - HALO:], 'dom', up)]
  transfers between devices with their start and end apart: 2 -> 0, of which waited for: 2 -> 0; matrix products, arithmetic and copies ran while one was open for 2% -> 0% of each run, Pallas kernels for 8% -> 0%
where the time goes in v3:
time: 139 us; the launch traced here: 137 us
  Pallas kernels  128 us (92%)
  local copies, waits for them, and re-layouts  6.46 us (5%)
  other arithmetic  1.47 us (1%)
    pallas_call x1, Pallas kernels, solve(): pl.pallas_call(solve_kernel, out_shape=(jax.ShapeDtypeStruct((SX, 2, NY,...  116 us
    pallas_call x1, Pallas kernels, build_table(): pl.pallas_call(table_kernel, out_shape=jax.ShapeDtypeStruct((SX * NY, 2 *...  12.5 us
    reshape x1, local copies, waits for them, and re-layouts, shards(): orb = orbitals.reshape(2, 8, SX, NY, NZ).transpose(2, 0, 3, 1, 4)  3.24 us

profile of v3, /device:TPU:1, one launch (start us, length us, event | category | flops | bytes accessed | tf_op | source)
XLA Modules:
  0.0 137.1 jit_solution(5852413122189375201)
XLA Ops:
  0.6 0.8 pad_dynamic-slice_fusion
  1.4 0.7 broadcast_subtract_fusion
  2.1 0.1 sub.19.lev
  2.1 0.8 add_select_fusion.place
  3.0 0.0 copy-start.3
  3.0 3.2 %copy.16 = f32[2,8,8,32,128]{4,1,3,0,2:T(8,128)S(1)} copy(f32[2,8,8,32,128]{4,3,2,1,0:T(8,128)} %bitcast.14) | data formatting | bytes 4194304 | tf_op jit(solution)/shard_map/reshape | solution.py:756
  6.2 0.0 copy-done.3
  6.2 0.0 copy-start
  6.2 0.0 copy-start.1
  6.2 0.0 copy-start.2
  6.3 12.5 %projector_table.1.table = bf16[256,96,128]{2,1,0:T(8,128)(2,1)S(1)} custom-call(s32[8224]{0:T(1024)S(1)} %add_select_fusion.place, f32[8224]{0:T(1024)S(1)} %copy-done.3), custom_call_target="tpu_custom_call" | custom-call | bytes 41943040 | tf_op jit(solution)/shard_map/projector_table/pallas_call | solution.py:98
  18.8 0.0 copy-done
  18.8 0.0 copy-done.1
  18.8 0.0 copy-done.2
  18.8 116.0 %bicg_solve.1 = (f32[8,2,32,8,128]{4,3,2,1,0:T(8,128)S(1)}, f32[8,8,128]{2,1,0:T(8,128)S(1)}) custom-call(bf16[256,96,128]{2,1,0:T(8,128)(2,1)S(1)} %projector_table.1.table, f32[8,2,32,8,128]{4,3,2,1,0:T(8,128)S(1)} %bitcast.10, f32[256,128]{1,0:T(8,128)S(1)} %bitcast.12, f32[256,128]{1,0:T(8,128)S(1)} %bitcast.13, f32[2,8,1]{2,1,0:T(8,128)S(1)} %sub.19.lev, ...), custom_call_target="tpu_custom_call" | custom-call | tf_op jit(solution)/shard_map/bicg_solve/pallas_call | solution.py:708
  134.8 1.7 %copy.14 = f32[2,8,8,32,128]{4,3,2,1,0:T(8,128)} copy(f32[2,8,8,32,128]{4,1,3,0,2:T(8,128)S(1)} %bitcast.11) | data formatting | bytes 4194304 | tf_op jit(solution)/shard_map/transpose | solution.py:770
  136.5 0.6 copy.18
  (1 shorter events, 0.0 us)
Async XLA Ops:
  3.0 3.3 %copy-start.3 = (f32[8224]{0:T(1024)S(1)}, f32[8224]{0:T(1024)}, u32[]{:S(2)}) copy-start(f32[8224]{0:T(1024)} %value.1) | copy-start | bytes 98692
  6.2 12.5 %copy-start = (f32[8,32,128]{2,1,0:T(8,128)S(1)}, f32[8,32,128]{2,1,0:T(8,128)}, u32[]{:S(2)}) copy-start(f32[8,32,128]{2,1,0:T(8,128)} %param.11) | copy-start | bytes 393220
  6.2 12.5 %copy-start.1 = (f32[8,32,128]{2,1,0:T(8,128)S(1)}, f32[8,32,128]{2,1,0:T(8,128)}, u32[]{:S(2)}) copy-start(f32[8,32,128]{2,1,0:T(8,128)} %param.12) | copy-start | bytes 393220
  6.2 12.5 %copy-start.2 = (bf16[256,256]{1,0:T(8,128)(2,1)S(1)}, bf16[256,256]{1,0:T(8,128)(2,1)}, u32[]{:S(2)}) copy-start(bf16[256,256]{1,0:T(8,128)(2,1)} %constant.32.clone.tz) | copy-start | bytes 393220

commit v4 on v3

--- a/solution.py
+++ b/solution.py
@@ -77,7 +77,7 @@
             pltpu.store(
                 dense.at[pl.ds(where >> 7, 1), :],
                 jnp.full((1, NZ), value[i * UNROLL + u], F32),
-                mask=lanes == (where & 127),
+                mask=lanes == (jnp.full((1, NZ), where, jnp.int32) & 127),
             )
         return 0
 
@@ -108,9 +108,9 @@
 
 
 def solve_kernel(
-    table, orb, pot_in, pert_in, lev, energy, tz,
+    table, orb, pot_in, pert_in, lev, kb, tz,
     x_out, dens_out,
-    own_in, turned, r, s, w, hb, hb2, hist, potb, st1, st2, pj, msg, pmsg, scal, tot, lhs, dens, parts,
+    energy, own_in, turned, r, s, w, hb, hb2, hist, potb, st1, st2, pj, msg, pmsg, scal, tot, lhs, dens, parts,
     h_send, h_recv, a_send, a_recv, b_send, b_recv, p_send, p_recv, d_send, d_recv,
 ):
     d = lax.axis_index("dom")
@@ -171,11 +171,13 @@
 
     near = ((-2, d >= 2), (-1, d >= 1), (1, d < N_DOM - 1), (2, d < N_DOM - 2))
 
-    def in_plane(i):
+    first_at, second_at = zi, ji
+
+    def in_first(i):
+        return ((zi + i) % DEPTH) * PLANE + ji
+
+    def in_second(i):
         return zi * PLANE + (ji + i) % PLANE
-
-    def in_column(i):
-        return ((zi + i) % DEPTH) * PLANE + ji
 
     me = lax.axis_index("st")
     blocks_st = lax.axis_size("st")
@@ -188,9 +190,9 @@
     for i in range(1, blocks_st):
         pl.semaphore_signal(barrier, inc=1, device_id={"st": other_block(i)})
     for i in range(1, PLANE):
-        pl.semaphore_signal(barrier, inc=1, device_id={"dom": in_plane(i)})
+        pl.semaphore_signal(barrier, inc=1, device_id={"dom": in_first(i)})
     for i in range(1, DEPTH):
-        pl.semaphore_signal(barrier, inc=1, device_id={"dom": in_column(i)})
+        pl.semaphore_signal(barrier, inc=1, device_id={"dom": in_second(i)})
     for step, there in near:
         count = count + there.astype(jnp.int32)
 
@@ -199,6 +201,11 @@
             pl.semaphore_signal(barrier, inc=1, device_id={"dom": d + step})
 
     lanes = lax.broadcasted_iota(jnp.int32, (8, NZ), 1)
+    line = jnp.zeros((1, NZ), F32)
+    for j in range(SLOTS):
+        atom = jnp.clip((d - 1) * ATOM_DEV + j, 0, kb.shape[0] - 1)
+        line = jnp.where(lanes[:1] == j, kb[atom], line)
+    energy[...] = line
 
     pl.semaphore_wait(barrier, count)
 
@@ -250,40 +257,40 @@
             total = total + jnp.where((lanes >= low) & (lanes < high), moved, 0.0)
         return total
 
-    def plane_copy(k, g, i):
+    def first_copy(k, g, i):
         return pltpu.make_async_remote_copy(
             src_ref=msg.at[k, g, 0],
-            dst_ref=st1.at[k, g, ji],
+            dst_ref=st1.at[k, g, first_at],
             send_sem=a_send.at[g, i],
             recv_sem=a_recv.at[k % 2, g, i],
-            device_id={"dom": in_plane(i)},
-        )
-
-    def plane_arrival(k, g, i):
+            device_id={"dom": in_first(i)},
+        )
+
+    def first_arrival(k, g, i):
         return pltpu.make_async_remote_copy(
             src_ref=msg.at[k, g, 0],
-            dst_ref=st1.at[k, g, (ji + PLANE - i) % PLANE],
+            dst_ref=st1.at[k, g, (first_at + PLANE - i) % PLANE],
             send_sem=a_send.at[g, i],
             recv_sem=a_recv.at[k % 2, g, i],
-            device_id={"dom": in_plane(i)},
-        )
-
-    def column_copy(k, g, i):
+            device_id={"dom": in_first(i)},
+        )
+
+    def second_copy(k, g, i):
         return pltpu.make_async_remote_copy(
             src_ref=msg.at[k, g, 1],
-            dst_ref=st2.at[k, g, zi],
+            dst_ref=st2.at[k, g, second_at],
             send_sem=b_send.at[g, i],
             recv_sem=b_recv.at[k % 2, g, i],
-            device_id={"dom": in_column(i)},
-        )
-
-    def column_arrival(k, g, i):
+            device_id={"dom": in_second(i)},
+        )
+
+    def second_arrival(k, g, i):
         return pltpu.make_async_remote_copy(
             src_ref=msg.at[k, g, 1],
-            dst_ref=st2.at[k, g, (zi + DEPTH - i) % DEPTH],
+            dst_ref=st2.at[k, g, (second_at + DEPTH - i) % DEPTH],
             send_sem=b_send.at[g, i],
             recv_sem=b_recv.at[k % 2, g, i],
-            device_id={"dom": in_column(i)},
+            device_id={"dom": in_second(i)},
         )
 
     def send_sums(k, g, rr, rw):
@@ -291,26 +298,26 @@
             lanes < 64, jnp.sum(rr, axis=1, keepdims=True), jnp.sum(rw, axis=1, keepdims=True)
         )
         msg[k, g, 0] = tile
-        st1[k, g, ji] = tile
+        st1[k, g, first_at] = tile
         for i in range(1, PLANE):
-            plane_copy(k, g, i).start()
+            first_copy(k, g, i).start()
 
     def forward_sums(k, g):
         for i in range(1, PLANE):
-            plane_arrival(k, g, i).wait_recv()
-            plane_copy(k, g, i).wait_send()
+            first_arrival(k, g, i).wait_recv()
+            first_copy(k, g, i).wait_send()
         tile = st1[k, g, 0]
         for i in range(1, PLANE):
             tile = tile + st1[k, g, i]
         msg[k, g, 1] = tile
-        st2[k, g, zi] = tile
+        st2[k, g, second_at] = tile
         for i in range(1, DEPTH):
-            column_copy(k, g, i).start()
+            second_copy(k, g, i).start()
 
     def take_sums(k, g):
         for i in range(1, DEPTH):
-            column_arrival(k, g, i).wait_recv()
-            column_copy(k, g, i).wait_send()
+            second_arrival(k, g, i).wait_recv()
+            second_copy(k, g, i).wait_send()
         tile = st2[k, g, 0]
         for i in range(1, DEPTH):
             tile = tile + st2[k, g, i]
@@ -466,7 +473,11 @@
     none = jnp.zeros((8, NZ), F32)
 
     def level_of(g):
-        return jnp.broadcast_to(lev[g], (8, NZ))
+        rows = lax.broadcasted_iota(jnp.int32, (8, NZ), 0)
+        value = none
+        for j in range(8):
+            value = jnp.where(rows == j, -1.5 * C[0] - lev[g * 8 + j], value)
+        return value
 
     def main(k, g, between):
         level = level_of(g)
@@ -482,10 +493,10 @@
             left = lhs[:, : 2 * SLOTS]
             for n, (f, image) in enumerate(zip(fs, images)):
                 row = x * NY + y0 + n * 8
-                blocks = []
-                for j in range(8):
-                    v = jnp.dot(left, table[row + j], preferred_element_type=F32)
-                    blocks.append(image[j] + (v[:8] + v[8:]))
+                right = jnp.concatenate([table[row + j] for j in range(8)], axis=1)
+                v = jnp.dot(left, right, preferred_element_type=F32)
+                v = v[:8] + v[8:]
+                blocks = [image[j] + v[:, j * NZ : (j + 1) * NZ] for j in range(8)]
                 for j in range(8):
                     w[k % 2, g, x, y0 + n * 8 + j] = blocks[j]
                 rr = rr + tree(f * f)
@@ -702,7 +713,7 @@
         block_copy(i, me).wait_send()
 
 
-def solve(table, orb, pot, pert, lev, energy, tz, blocks_st):
+def solve(table, orb, pot, pert, lev, kb, tz, blocks_st):
     vmem = pl.BlockSpec(memory_space=pltpu.VMEM)
     dma = pltpu.SemaphoreType.DMA
     return pl.pallas_call(
@@ -711,9 +722,10 @@
             jax.ShapeDtypeStruct((SX, 2, NY, 8, NZ), F32),
             jax.ShapeDtypeStruct((SX, NY // blocks_st, NZ), F32),
         ),
-        in_specs=[vmem] * 7,
+        in_specs=[vmem] * 4 + [pl.BlockSpec(memory_space=pltpu.SMEM)] * 2 + [vmem],
         out_specs=(vmem, vmem),
         scratch_shapes=[
+            pltpu.VMEM((1, NZ), F32),
             pltpu.VMEM((SX, 2, NY, 8, NZ), F32),
             pltpu.VMEM((SX * NY * NZ, 2 * SLOTS), BF16),
             pltpu.VMEM((2, EXT, NYP, 8, NZ), F32),
@@ -748,7 +760,7 @@
             collective_id=0, has_side_effects=True, vmem_limit_bytes=VMEM_MIB * 2**20
         ),
         name="bicg_solve",
-    )(table, orb, pot, pert, lev, energy, tz)
+    )(table, orb, pot, pert, lev, kb, tz)
 
 
 def shards(orbitals, levels, potential, perturbation, projector, point_cell, point_atom, kb_energy):
@@ -757,14 +769,10 @@
     row = (point_cell >> 7) * SLOTS + point_atom - (index - 1) * ATOM_DEV
     place = jnp.where(point_atom >= 0, row * NZ + (point_cell & 127), UNUSED)
     table = build_table(projector, place)
-    energy = lax.dynamic_slice_in_dim(
-        jnp.pad(kb_energy, (ATOM_DEV, ATOM_DEV)), index * ATOM_DEV, SLOTS
-    )
-    energy = jnp.pad(energy, (0, NZ - SLOTS))[None]
-    lev = (-1.5 * C[0]) - levels.reshape(2, 8, 1)
     tz = jnp.asarray(depth_matrix())
     turned, density = solve(
-        table, orb, potential.reshape(SX * NY, NZ), perturbation.reshape(SX * NY, NZ), lev, energy, tz,
+        table, orb, potential.reshape(SX * NY, NZ), perturbation.reshape(SX * NY, NZ),
+        levels, kb_energy, tz,
         lax.axis_size("st"),
     )
     response = turned.transpose(1, 3, 0, 2, 4).reshape(orbitals.shape)

time: 139 us -> 130 us (0.935); the launches traced: 137 us -> 130 us
  Pallas kernels: 128 us -> 123 us
    pallas_call x1, Pallas kernels: 116 us -> 112 us  [solve(): pl.pallas_call(solve_kernel, out_shape=(jax.ShapeDtypeStruct((SX, 2, NY,...]
    pallas_call x1, Pallas kernels: 12.5 us -> 10.8 us  [build_table(): pl.pallas_call(table_kernel, out_shape=jax.ShapeDtypeStruct((SX * NY, 2 *...]
where the time goes in v4:
time: 130 us
  Pallas kernels  123 us (95%)
  local copies, waits for them, and re-layouts  5.61 us (4%)
    pallas_call x1, Pallas kernels, solve(): pl.pallas_call(solve_kernel, out_shape=(jax.ShapeDtypeStruct((SX, 2, NY,...  112 us
    pallas_call x1, Pallas kernels, build_table(): pl.pallas_call(table_kernel, out_shape=jax.ShapeDtypeStruct((SX * NY, 2 *...  10.8 us
    reshape x1, local copies, waits for them, and re-layouts, shards(): orb = orbitals.reshape(2, 8, SX, NY, NZ).transpose(2, 0, 3, 1, 4)  3.24 us

profile of v4, /device:TPU:1, one launch (start us, length us, event | category | flops | bytes accessed | tf_op | source)
XLA Modules:
  0.0 130.3 jit_solution(8736352460462048165)
XLA Ops:
  0.6 0.8 add_select_fusion.place
  1.4 0.0 copy-start.3
  1.5 3.2 %copy.14 = f32[2,8,8,32,128]{4,1,3,0,2:T(8,128)S(1)} copy(f32[2,8,8,32,128]{4,3,2,1,0:T(8,128)} %bitcast.12) | data formatting | bytes 4194304 | tf_op jit(solution)/shard_map/reshape | solution.py:768
  4.7 0.0 copy-done.3
  4.7 0.0 copy-start
  4.7 0.0 copy-start.1
  4.7 0.0 copy-start.2
  4.7 0.0 copy-start.4
  4.8 0.0 copy-start.5
  4.8 10.8 %projector_table.1.table = bf16[256,96,128]{2,1,0:T(8,128)(2,1)S(1)} custom-call(s32[8224]{0:T(1024)S(1)} %add_select_fusion.place, f32[8224]{0:T(1024)S(1)} %copy-done.3), custom_call_target="tpu_custom_call" | custom-call | bytes 41943040 | tf_op jit(solution)/shard_map/projector_table/pallas_call | solution.py:98
  15.5 0.0 copy-done
  15.5 0.0 copy-done.1
  15.5 0.0 copy-done.2
  15.6 0.0 copy-done.4
  15.6 0.0 copy-done.5
  15.6 112.4 %bicg_solve.1 = (f32[8,2,32,8,128]{4,3,2,1,0:T(8,128)S(1)}, f32[8,8,128]{2,1,0:T(8,128)S(1)}) custom-call(bf16[256,96,128]{2,1,0:T(8,128)(2,1)S(1)} %projector_table.1.table, f32[8,2,32,8,128]{4,3,2,1,0:T(8,128)S(1)} %bitcast.8, f32[256,128]{1,0:T(8,128)S(1)} %bitcast.10, f32[256,128]{1,0:T(8,128)S(1)} %bitcast.11, f32[16]{0:T(128)S(1)} %copy-done.5, ...), custom_call_target="tpu_custom_call" | custom-call | tf_op jit(solution)/shard_map/bicg_solve/pallas_call | solution.py:719
  128.0 1.7 %copy.12 = f32[2,8,8,32,128]{4,3,2,1,0:T(8,128)} copy(f32[2,8,8,32,128]{4,1,3,0,2:T(8,128)S(1)} %bitcast.9) | data formatting | bytes 4194304 | tf_op jit(solution)/shard_map/transpose | solution.py:778
  129.7 0.6 copy.16
Async XLA Ops:
  1.4 3.3 %copy-start.3 = (f32[8224]{0:T(1024)S(1)}, f32[8224]{0:T(1024)}, u32[]{:S(2)}) copy-start(f32[8224]{0:T(1024)} %value.1) | copy-start | bytes 98692
  4.7 10.8 %copy-start = (f32[8,32,128]{2,1,0:T(8,128)S(1)}, f32[8,32,128]{2,1,0:T(8,128)}, u32[]{:S(2)}) copy-start(f32[8,32,128]{2,1,0:T(8,128)} %param.11) | copy-start | bytes 393220
  4.7 10.8 %copy-start.1 = (f32[8,32,128]{2,1,0:T(8,128)S(1)}, f32[8,32,128]{2,1,0:T(8,128)}, u32[]{:S(2)}) copy-start(f32[8,32,128]{2,1,0:T(8,128)} %param.12) | copy-start | bytes 393220
  4.7 10.8 %copy-start.2 = (bf16[256,256]{1,0:T(8,128)(2,1)S(1)}, bf16[256,256]{1,0:T(8,128)(2,1)}, u32[]{:S(2)}) copy-start(bf16[256,256]{1,0:T(8,128)(2,1)} %constant.25.clone.tz) | copy-start | bytes 393220
  4.7 10.8 %copy-start.4 = (f32[1024]{0:T(1024)S(1)}, f32[1024]{0:T(1024)}, u32[]{:S(2)}) copy-start(f32[1024]{0:T(1024)} %kb.1) | copy-start | bytes 12292
  4.8 10.8 %copy-start.5 = (f32[16]{0:T(128)S(1)}, f32[16]{0:T(128)}, u32[]{:S(2)}) copy-start(f32[16]{0:T(128)} %lev.1) | copy-start | bytes 196

commit v5 on v4

--- a/solution.py
+++ b/solution.py
@@ -10,6 +10,7 @@
 SLOTS = 3 * ATOM_DEV
 SX, NY, NZ = 8, 32, 128
 HALO = 6
+HALF = HALO // 2
 EXT = SX + 2 * HALO
 NYP = NY + 2 * HALO
 N_DOM = 64
@@ -49,7 +50,13 @@
     return jnp.concatenate([high, value - high], axis=axis).astype(BF16)
 
 
-def table_kernel(place, value, table, dense):
+def table_kernel(place, value, orb, table, turned, dense, sems):
+    moves = [
+        pltpu.make_async_copy(orb.at[n], turned.at[:, n // 8, :, n % 8, :], sems.at[n])
+        for n in range(16)
+    ]
+    for c in moves:
+        c.start()
     slots = place.shape[0]
 
     def clear(i, _):
@@ -91,20 +98,28 @@
         return 0
 
     lax.fori_loop(0, SX * NY // 4, split, 0)
-
-
-def build_table(projector, place):
+    for c in moves:
+        c.wait()
+
+
+def build_table(projector, place, orbitals):
     smem = pl.BlockSpec(memory_space=pltpu.SMEM)
     return pl.pallas_call(
         table_kernel,
-        out_shape=jax.ShapeDtypeStruct((SX * NY, 2 * SLOTS, NZ), BF16),
-        in_specs=[smem, smem],
-        out_specs=pl.BlockSpec(memory_space=pltpu.VMEM),
-        scratch_shapes=[pltpu.VMEM((SX * NY * SLOTS + 8, NZ), F32)],
+        out_shape=(
+            jax.ShapeDtypeStruct((SX * NY, 2 * SLOTS, NZ), BF16),
+            jax.ShapeDtypeStruct((SX, 2, NY, 8, NZ), F32),
+        ),
+        in_specs=[smem, smem, pl.BlockSpec(memory_space=pl.ANY)],
+        out_specs=(pl.BlockSpec(memory_space=pltpu.VMEM), pl.BlockSpec(memory_space=pltpu.VMEM)),
+        scratch_shapes=[
+            pltpu.VMEM((SX * NY * SLOTS + 8, NZ), F32),
+            pltpu.SemaphoreType.DMA((16,)),
+        ],
         compiler_params=pltpu.CompilerParams(vmem_limit_bytes=10 * 2**20),
         cost_estimate=pl.CostEstimate(flops=0, bytes_accessed=40 * 2**20, transcendentals=0),
         name="projector_table",
-    )(place, projector)
+    )(place, projector, orbitals)
 
 
 def solve_kernel(
@@ -334,9 +349,10 @@
         return alpha, beta
 
     def up_copy(k, g):
-        dst = hb.at[k, g, pl.ds(0, HALO)] if k < 2 else hb2.at[g]
-        return pltpu.make_async_remote_copy(
-            src_ref=w.at[k % 2, g, pl.ds(SX - HALO, HALO)],
+        planes = HALO if k < 2 else HALF
+        dst = hb.at[k, g, pl.ds(0, HALO)] if k < 2 else hb2.at[g, pl.ds(0, HALF)]
+        return pltpu.make_async_remote_copy(
+            src_ref=w.at[k % 2, g, pl.ds(SX - planes, planes)],
             dst_ref=dst,
             send_sem=h_send.at[k, g, 0],
             recv_sem=h_recv.at[k, g, 0],
@@ -344,9 +360,10 @@
         )
 
     def down_copy(k, g):
-        dst = hb.at[k, g, pl.ds(HALO, HALO)] if k < 2 else hb2.at[g]
-        return pltpu.make_async_remote_copy(
-            src_ref=w.at[k % 2, g, pl.ds(0, HALO)],
+        planes = HALO if k < 2 else HALF
+        dst = hb.at[k, g, pl.ds(HALO, HALO)] if k < 2 else hb2.at[g, pl.ds(HALF, HALF)]
+        return pltpu.make_async_remote_copy(
+            src_ref=w.at[k % 2, g, pl.ds(0, planes)],
             dst_ref=dst,
             send_sem=h_send.at[k, g, 1],
             recv_sem=h_recv.at[k, g, 1],
@@ -354,16 +371,16 @@
         )
 
     def goes_up(k, g):
-        return (d < N_DOM - 1) if k < 2 else ((d < N_DOM - 1) & (g == 0))
+        return d < N_DOM - 1
 
     def goes_down(k, g):
-        return (d > 0) if k < 2 else ((d > 0) & (g == 1))
+        return d > 0
 
     def comes_up(k, g):
-        return (d > 0) if k < 2 else ((d > 0) & (g == 0))
+        return d > 0
 
     def comes_down(k, g):
-        return (d < N_DOM - 1) if k < 2 else ((d < N_DOM - 1) & (g == 1))
+        return d < N_DOM - 1
 
     def send_halo(k, g):
         @pl.when(goes_up(k, g))
@@ -486,7 +503,7 @@
         lhs[...] = both_parts(coeff, 0)
 
         def body(i, carry):
-            rr, rw, acc = carry
+            rr, rw = carry
             pl.when(i == BREAK)(between)
             x, y0 = place(i)
             fs, images = stencil(g, x, y0, level, ROWS)
@@ -501,15 +518,22 @@
                     w[k % 2, g, x, y0 + n * 8 + j] = blocks[j]
                 rr = rr + tree(f * f)
                 rw = rw + tree([f[j] * blocks[j] for j in range(8)])
-                acc = project(blocks, row, acc)
-            return rr, rw, acc
-
-        rr, rw, acc = lax.fori_loop(
-            0, SX * NY // ROWS, body, (none, none, jnp.zeros((16, 2 * SLOTS), F32))
-        )
+            return rr, rw
+
+        rr, rw = lax.fori_loop(0, SX * NY // ROWS, body, (none, none))
         send_sums(k, g, rr, rw)
+        send_halo(k, g)
+
+        def images(i, acc):
+            x = i // 2
+            y0 = pl.multiple_of((i % 2) * 16, 16)
+            for n in range(2):
+                blocks = [w[k % 2, g, x, y0 + n * 8 + j] for j in range(8)]
+                acc = project(blocks, x * NY + y0 + n * 8, acc)
+            return acc
+
+        acc = lax.fori_loop(0, SX * NY // 16, images, jnp.zeros((16, 2 * SLOTS), F32))
         send_projections(k + 1, g, acc)
-        send_halo(k, g)
 
     def last(g):
         level = level_of(g)
@@ -517,6 +541,12 @@
         def body(i, carry):
             rr, rw = carry
             x, y0 = place(i)
+
+            @pl.when(x == SX - HALF)
+            def _():
+                for j in range(HALF):
+                    r[g, SX + HALO + j, inner] = jnp.zeros((NY, 8, NZ), F32)
+
             for f, image in zip(*stencil(g, x, y0, level, ROWS)):
                 rr, rw = rr + tree(f * f), rw + tree(f * image)
             return rr, rw
@@ -529,11 +559,6 @@
 
     def update(k, g):
         alpha, beta = take_sums(k - 1, g)
-        t = gathered_projections(k, g)
-        if k > 1:
-            t = t + beta * tot[g, 1]
-        tot[g, 1] = t
-        tot[g, 0] = tot[g, 0] - alpha * t
         a, b = alpha[None], beta[None]
 
         def own(i, _):
@@ -568,19 +593,31 @@
 
             lax.fori_loop(0, 2 * HALO * 4, side, 0)
         else:
-            base = jnp.where(g == 0, 0, HALO + SX)
-            other = HALO + SX - base
-
-            def one_side(i, _):
+            def near_side(i, _):
                 x = i // 4
                 y0 = pl.multiple_of((i % 4) * 8, 8)
-                step = hb2[g, x, pl.ds(y0, 8)] + b * s[g, base + x, pl.ds(y0, 8)]
-                new = r[g, base + x, pl.ds(y0 + HALO, 8)] - a * step
-                r[g, base + x, pl.ds(y0 + HALO, 8)] = new + new
-                r[g, other + x, pl.ds(y0 + HALO, 8)] = jnp.zeros((8, 8, NZ), F32)
+                to = jnp.where(x < HALF, x + HALF, x + SX + HALO - HALF)
+                step = hb2[g, x, pl.ds(y0, 8)] + b * s[g, to, pl.ds(y0, 8)]
+                new = r[g, to, pl.ds(y0 + HALO, 8)] - a * step
+                r[g, to, pl.ds(y0 + HALO, 8)] = new + new
                 return 0
 
-            lax.fori_loop(0, HALO * 4, one_side, 0)
+            lax.fori_loop(0, 2 * HALF * 4, near_side, 0)
+
+            def far_side(i, _):
+                plane = jnp.zeros((NY, 8, NZ), F32)
+                r[g, i, inner] = plane
+                r[g, EXT - 1 - i, inner] = plane
+                return 0
+
+            lax.fori_loop(0, HALF, far_side, 0)
+
+    def update_projections(k, g):
+        t = gathered_projections(k, g)
+        if k > 1:
+            t = t + scal[g, 3 + k] * tot[g, 1]
+        tot[g, 1] = t
+        tot[g, 0] = tot[g, 0] - scal[g, k - 1] * t
 
     def each(body):
         def run(g, _):
@@ -642,6 +679,7 @@
 
         def turn(g, k=k):
             update(k, g)
+            update_projections(k, g)
             main(k, g, lambda: pass_on(k, g))
 
         each(turn)
@@ -651,6 +689,7 @@
 
     def closing(g):
         update(3, g)
+        update_projections(3, g)
         pass_on(3, g)
         last(g)
 
@@ -765,10 +804,9 @@
 
 def shards(orbitals, levels, potential, perturbation, projector, point_cell, point_atom, kb_energy):
     index = lax.axis_index("dom")
-    orb = orbitals.reshape(2, 8, SX, NY, NZ).transpose(2, 0, 3, 1, 4)
     row = (point_cell >> 7) * SLOTS + point_atom - (index - 1) * ATOM_DEV
     place = jnp.where(point_atom >= 0, row * NZ + (point_cell & 127), UNUSED)
-    table = build_table(projector, place)
+    table, orb = build_table(projector, place, orbitals)
     tz = jnp.asarray(depth_matrix())
     turned, density = solve(
         table, orb, potential.reshape(SX * NY, NZ), perturbation.reshape(SX * NY, NZ),

time: 130 us -> 121 us (0.931)
  Pallas kernels: 123 us -> 115 us
    pallas_call x1, Pallas kernels: 112 us -> 102 us  [solve(): pl.pallas_call(solve_kernel, out_shape=(jax.ShapeDtypeStruct((SX, 2, NY,...]
    reshape x1 -> x0, local copies, waits for them, and re-layouts: 3.24 us -> none  [shards(): orb = orbitals.reshape(2, 8, SX, NY, NZ).transpose(2, 0, 3, 1, 4)]
    unnamed x13 -> x15, local copies, waits for them, and re-layouts: 0.65 us -> 2.99 us
    pallas_call x1, Pallas kernels: 10.8 us -> 12.9 us  [build_table(): pl.pallas_call(table_kernel, out_shape=(jax.ShapeDtypeStruct((SX * NY, 2...]
where the time goes in v5:
time: 121 us
  Pallas kernels  115 us (95%)
  local copies, waits for them, and re-layouts  4.71 us (4%)
    pallas_call x1, Pallas kernels, solve(): pl.pallas_call(solve_kernel, out_shape=(jax.ShapeDtypeStruct((SX, 2, NY,...  102 us
    pallas_call x1, Pallas kernels, build_table(): pl.pallas_call(table_kernel, out_shape=(jax.ShapeDtypeStruct((SX * NY, 2...  12.9 us
    unnamed x15, local copies, waits for them, and re-layouts  2.99 us

profile of v5, /device:TPU:1, one launch (start us, length us, event | category | flops | bytes accessed | tf_op | source)
XLA Modules:
  0.0 121.1 jit_solution(15673166914706997762)
XLA Ops:
  0.6 0.0 copy-start.5
  0.6 0.0 copy-start.6
  0.7 0.8 add_select_fusion.place
  1.5 0.0 copy-start
  1.5 1.6 %copy-done = f32[16,8,32,128]{3,2,1,0:T(8,128)S(1)} copy-done((f32[16,8,32,128]{3,2,1,0:T(8,128)S(1)}, f32[16,8,32,128]{3,2,1,0:T(8,128)}, u32[]{:S(2)}) %copy-start) | copy-done | bytes 2097176
  3.1 0.0 copy-start.4
  3.1 0.8 copy-done.4
  3.8 0.0 copy-start.1
  3.8 0.0 copy-start.2
  3.8 0.0 copy-start.3
  3.8 12.9 %projector_table.1 = (bf16[256,96,128]{2,1,0:T(8,128)(2,1)S(1)}, f32[8,2,32,8,128]{4,3,2,1,0:T(8,128)S(1)}) custom-call(s32[8224]{0:T(1024)S(1)} %add_select_fusion.place, f32[8224]{0:T(1024)S(1)} %copy-done.4, f32[16,8,32,128]{3,2,1,0:T(8,128)S(1)} %copy-done), custom_call_target="tpu_custom_call" | custom-call | bytes 41943040 | tf_op jit(solution)/shard_map/projector_table/pallas_call | solution.py:107
  16.7 0.0 copy-done.5
  16.8 0.0 copy-done.6
  16.8 0.0 copy-done.1
  16.8 0.0 copy-done.2
  16.8 0.0 copy-done.3
  16.8 102.0 %bicg_solve.1 = (f32[8,2,32,8,128]{4,3,2,1,0:T(8,128)S(1)}, f32[8,8,128]{2,1,0:T(8,128)S(1)}) custom-call(bf16[256,96,128]{2,1,0:T(8,128)(2,1)S(1)} %get-tuple-element.6.table, f32[8,2,32,8,128]{4,3,2,1,0:T(8,128)S(1)} %get-tuple-element.7.orb, f32[256,128]{1,0:T(8,128)S(1)} %bitcast.5, f32[256,128]{1,0:T(8,128)S(1)} %bitcast.6, f32[16]{0:T(128)S(1)} %copy-done.6, ...), custom_call_target="tpu_custom_call" | custom-call | tf_op jit(solution)/shard_map/bicg_solve/pallas_call | solution.py:758
  118.8 1.7 %copy.11 = f32[2,8,8,32,128]{4,3,2,1,0:T(8,128)} copy(f32[2,8,8,32,128]{4,1,3,0,2:T(8,128)S(1)} %bitcast.4) | data formatting | bytes 4194304 | tf_op jit(solution)/shard_map/transpose | solution.py:816
  120.5 0.6 copy.13
Async XLA Ops:
  0.6 16.1 %copy-start.5 = (f32[1024]{0:T(1024)S(1)}, f32[1024]{0:T(1024)}, u32[]{:S(2)}) copy-start(f32[1024]{0:T(1024)} %kb.1) | copy-start | bytes 12292
  0.6 16.1 %copy-start.6 = (f32[16]{0:T(128)S(1)}, f32[16]{0:T(128)}, u32[]{:S(2)}) copy-start(f32[16]{0:T(128)} %lev.1) | copy-start | bytes 196
  1.5 1.6 %copy-start = (f32[16,8,32,128]{3,2,1,0:T(8,128)S(1)}, f32[16,8,32,128]{3,2,1,0:T(8,128)}, u32[]{:S(2)}) copy-start(f32[16,8,32,128]{3,2,1,0:T(8,128)} %orb.1) | copy-start | bytes 6291460
  3.1 0.8 copy-start.4
  3.8 12.9 %copy-start.1 = (f32[8,32,128]{2,1,0:T(8,128)S(1)}, f32[8,32,128]{2,1,0:T(8,128)}, u32[]{:S(2)}) copy-start(f32[8,32,128]{2,1,0:T(8,128)} %param.11) | copy-start | bytes 393220
  3.8 12.9 %copy-start.2 = (f32[8,32,128]{2,1,0:T(8,128)S(1)}, f32[8,32,128]{2,1,0:T(8,128)}, u32[]{:S(2)}) copy-start(f32[8,32,128]{2,1,0:T(8,128)} %param.12) | copy-start | bytes 393220
  3.8 12.9 %copy-start.3 = (bf16[256,256]{1,0:T(8,128)(2,1)S(1)}, bf16[256,256]{1,0:T(8,128)(2,1)}, u32[]{:S(2)}) copy-start(bf16[256,256]{1,0:T(8,128)(2,1)} %constant.25.clone.tz) | copy-start | bytes 393220

commit v6 on v5

--- a/solution.py
+++ b/solution.py
@@ -27,7 +27,7 @@
 )
 F32 = jnp.float32
 BF16 = jnp.bfloat16
-UNROLL = 8
+UNROLL = 16
 VMEM_MIB = 43
 ROWS = 32
 BREAK = 2
@@ -110,7 +110,7 @@
             jax.ShapeDtypeStruct((SX * NY, 2 * SLOTS, NZ), BF16),
             jax.ShapeDtypeStruct((SX, 2, NY, 8, NZ), F32),
         ),
-        in_specs=[smem, smem, pl.BlockSpec(memory_space=pl.ANY)],
+        in_specs=[smem, smem, pl.BlockSpec(memory_space=pltpu.HBM)],
         out_specs=(pl.BlockSpec(memory_space=pltpu.VMEM), pl.BlockSpec(memory_space=pltpu.VMEM)),
         scratch_shapes=[
             pltpu.VMEM((SX * NY * SLOTS + 8, NZ), F32),
@@ -132,6 +132,41 @@
     zi = d // PLANE
     ji = d % PLANE
     inner = pl.ds(HALO, NY)
+
+    for k in range(4):
+        for g in range(2):
+            pj[k, g] = jnp.zeros((4, 8, NZ), F32)
+
+    near = ((-2, d >= 2), (-1, d >= 1), (1, d < N_DOM - 1), (2, d < N_DOM - 2))
+
+    first_at, second_at = zi, ji
+
+    def in_first(i):
+        return ((zi + i) % DEPTH) * PLANE + ji
+
+    def in_second(i):
+        return zi * PLANE + (ji + i) % PLANE
+
+    me = lax.axis_index("st")
+    blocks_st = lax.axis_size("st")
+
+    def other_block(i):
+        return (me + i) % blocks_st
+
+    barrier = pltpu.get_barrier_semaphore()
+    count = jnp.int32(PLANE - 1 + DEPTH - 1 + blocks_st - 1)
+    for i in range(1, blocks_st):
+        pl.semaphore_signal(barrier, inc=1, device_id={"st": other_block(i)})
+    for i in range(1, PLANE):
+        pl.semaphore_signal(barrier, inc=1, device_id={"dom": in_first(i)})
+    for i in range(1, DEPTH):
+        pl.semaphore_signal(barrier, inc=1, device_id={"dom": in_second(i)})
+    for step, there in near:
+        count = count + there.astype(jnp.int32)
+
+        @pl.when(there)
+        def _(step=step):
+            pl.semaphore_signal(barrier, inc=1, device_id={"dom": d + step})
 
     zero = jnp.zeros((HALO, 8, NZ), F32)
 
@@ -179,41 +214,6 @@
     @pl.when(d == N_DOM - 1)
     def _():
         clear_halo(HALO)
-
-    for k in range(4):
-        for g in range(2):
-            pj[k, g] = jnp.zeros((4, 8, NZ), F32)
-
-    near = ((-2, d >= 2), (-1, d >= 1), (1, d < N_DOM - 1), (2, d < N_DOM - 2))
-
-    first_at, second_at = zi, ji
-
-    def in_first(i):
-        return ((zi + i) % DEPTH) * PLANE + ji
-
-    def in_second(i):
-        return zi * PLANE + (ji + i) % PLANE
-
-    me = lax.axis_index("st")
-    blocks_st = lax.axis_size("st")
-
-    def other_block(i):
-        return (me + i) % blocks_st
-
-    barrier = pltpu.get_barrier_semaphore()
-    count = jnp.int32(PLANE - 1 + DEPTH - 1 + blocks_st - 1)
-    for i in range(1, blocks_st):
-        pl.semaphore_signal(barrier, inc=1, device_id={"st": other_block(i)})
-    for i in range(1, PLANE):
-        pl.semaphore_signal(barrier, inc=1, device_id={"dom": in_first(i)})
-    for i in range(1, DEPTH):
-        pl.semaphore_signal(barrier, inc=1, device_id={"dom": in_second(i)})
-    for step, there in near:
-        count = count + there.astype(jnp.int32)
-
-        @pl.when(there)
-        def _(step=step):
-            pl.semaphore_signal(barrier, inc=1, device_id={"dom": d + step})
 
     lanes = lax.broadcasted_iota(jnp.int32, (8, NZ), 1)
     line = jnp.zeros((1, NZ), F32)

time: 121 us -> 119 us (0.983)
  Pallas kernels: 115 us -> 113 us
    pallas_call x1, Pallas kernels: 12.9 us -> 11.4 us  [build_table(): pl.pallas_call(table_kernel, out_shape=(jax.ShapeDtypeStruct((SX * NY, 2...]
where the time goes in v6:
time: 119 us; the launch traced here: 120 us
  Pallas kernels  113 us (95%)
  local copies, waits for them, and re-layouts  4.71 us (4%)
    pallas_call x1, Pallas kernels, solve(): pl.pallas_call(solve_kernel, out_shape=(jax.ShapeDtypeStruct((SX, 2, NY,...  102 us
    pallas_call x1, Pallas kernels, build_table(): pl.pallas_call(table_kernel, out_shape=(jax.ShapeDtypeStruct((SX * NY, 2...  11.4 us
    unnamed x15, local copies, waits for them, and re-layouts  2.99 us

profile of v6, /device:TPU:1, one launch (start us, length us, event | category | flops | bytes accessed | tf_op | source)
XLA Modules:
  0.0 119.6 jit_solution(7842650516541394286)
XLA Ops:
  0.6 0.0 copy-start.5
  0.6 0.0 copy-start.6
  0.7 0.8 add_select_fusion.place
  1.5 0.0 copy-start
  1.5 1.6 %copy-done = f32[16,8,32,128]{3,2,1,0:T(8,128)S(1)} copy-done((f32[16,8,32,128]{3,2,1,0:T(8,128)S(1)}, f32[16,8,32,128]{3,2,1,0:T(8,128)}, u32[]{:S(2)}) %copy-start) | copy-done | bytes 2097176
  3.1 0.0 copy-start.4
  3.1 0.8 copy-done.4
  3.8 0.0 copy-start.1
  3.8 0.0 copy-start.2
  3.8 0.0 copy-start.3
  3.8 11.4 %projector_table.1 = (bf16[256,96,128]{2,1,0:T(8,128)(2,1)S(1)}, f32[8,2,32,8,128]{4,3,2,1,0:T(8,128)S(1)}) custom-call(s32[8224]{0:T(1024)S(1)} %add_select_fusion.place, f32[8224]{0:T(1024)S(1)} %copy-done.4, f32[16,8,32,128]{3,2,1,0:T(8,128)S(1)} %copy-done), custom_call_target="tpu_custom_call" | custom-call | bytes 41943040 | tf_op jit(solution)/shard_map/projector_table/pallas_call | solution.py:107
  15.2 0.0 copy-done.5
  15.3 0.0 copy-done.6
  15.3 0.0 copy-done.1
  15.3 0.0 copy-done.2
  15.3 0.0 copy-done.3
  15.3 101.9 %bicg_solve.1 = (f32[8,2,32,8,128]{4,3,2,1,0:T(8,128)S(1)}, f32[8,8,128]{2,1,0:T(8,128)S(1)}) custom-call(bf16[256,96,128]{2,1,0:T(8,128)(2,1)S(1)} %get-tuple-element.6.table, f32[8,2,32,8,128]{4,3,2,1,0:T(8,128)S(1)} %get-tuple-element.7.orb, f32[256,128]{1,0:T(8,128)S(1)} %bitcast.5, f32[256,128]{1,0:T(8,128)S(1)} %bitcast.6, f32[16]{0:T(128)S(1)} %copy-done.6, ...), custom_call_target="tpu_custom_call" | custom-call | tf_op jit(solution)/shard_map/bicg_solve/pallas_call | solution.py:758
  117.2 1.7 %copy.11 = f32[2,8,8,32,128]{4,3,2,1,0:T(8,128)} copy(f32[2,8,8,32,128]{4,1,3,0,2:T(8,128)S(1)} %bitcast.4) | data formatting | bytes 4194304 | tf_op jit(solution)/shard_map/transpose | solution.py:816
  118.9 0.6 copy.13
Async XLA Ops:
  0.6 14.6 %copy-start.5 = (f32[1024]{0:T(1024)S(1)}, f32[1024]{0:T(1024)}, u32[]{:S(2)}) copy-start(f32[1024]{0:T(1024)} %kb.1) | copy-start | bytes 12292
  0.6 14.6 %copy-start.6 = (f32[16]{0:T(128)S(1)}, f32[16]{0:T(128)}, u32[]{:S(2)}) copy-start(f32[16]{0:T(128)} %lev.1) | copy-start | bytes 196
  1.5 1.6 %copy-start = (f32[16,8,32,128]{3,2,1,0:T(8,128)S(1)}, f32[16,8,32,128]{3,2,1,0:T(8,128)}, u32[]{:S(2)}) copy-start(f32[16,8,32,128]{3,2,1,0:T(8,128)} %orb.1) | copy-start | bytes 6291460
  3.1 0.8 copy-start.4
  3.8 11.4 %copy-start.1 = (f32[8,32,128]{2,1,0:T(8,128)S(1)}, f32[8,32,128]{2,1,0:T(8,128)}, u32[]{:S(2)}) copy-start(f32[8,32,128]{2,1,0:T(8,128)} %param.11) | copy-start | bytes 393220
  3.8 11.4 %copy-start.2 = (f32[8,32,128]{2,1,0:T(8,128)S(1)}, f32[8,32,128]{2,1,0:T(8,128)}, u32[]{:S(2)}) copy-start(f32[8,32,128]{2,1,0:T(8,128)} %param.12) | copy-start | bytes 393220
  3.8 11.4 %copy-start.3 = (bf16[256,256]{1,0:T(8,128)(2,1)S(1)}, bf16[256,256]{1,0:T(8,128)(2,1)}, u32[]{:S(2)}) copy-start(bf16[256,256]{1,0:T(8,128)(2,1)} %constant.25.clone.tz) | copy-start | bytes 393220

commit v7 on v6

--- a/solution.py
+++ b/solution.py
@@ -27,7 +27,7 @@
 )
 F32 = jnp.float32
 BF16 = jnp.bfloat16
-UNROLL = 16
+UNROLL = 32
 VMEM_MIB = 43
 ROWS = 32
 BREAK = 2
@@ -525,14 +525,12 @@
         send_halo(k, g)
 
         def images(i, acc):
-            x = i // 2
-            y0 = pl.multiple_of((i % 2) * 16, 16)
-            for n in range(2):
-                blocks = [w[k % 2, g, x, y0 + n * 8 + j] for j in range(8)]
-                acc = project(blocks, x * NY + y0 + n * 8, acc)
+            for n in range(4):
+                blocks = [w[k % 2, g, i, n * 8 + j] for j in range(8)]
+                acc = project(blocks, i * NY + n * 8, acc)
             return acc
 
-        acc = lax.fori_loop(0, SX * NY // 16, images, jnp.zeros((16, 2 * SLOTS), F32))
+        acc = lax.fori_loop(0, SX, images, jnp.zeros((16, 2 * SLOTS), F32))
         send_projections(k + 1, g, acc)
 
     def last(g):

time: 119 us -> 119 us (level)
  no operation moved by 1% of the time
where the time goes in v7:
time: 119 us
  Pallas kernels  113 us (95%)
  local copies, waits for them, and re-layouts  4.71 us (4%)
    pallas_call x1, Pallas kernels, solve(): pl.pallas_call(solve_kernel, out_shape=(jax.ShapeDtypeStruct((SX, 2, NY,...  101 us
    pallas_call x1, Pallas kernels, build_table(): pl.pallas_call(table_kernel, out_shape=(jax.ShapeDtypeStruct((SX * NY, 2...  11.2 us
    unnamed x15, local copies, waits for them, and re-layouts  2.99 us

profile of v7, /device:TPU:1, one launch (start us, length us, event | category | flops | bytes accessed | tf_op | source)
XLA Modules:
  0.0 118.8 jit_solution(13739713526306621037)
XLA Ops:
  0.6 0.0 copy-start.5
  0.6 0.0 copy-start.6
  0.7 0.8 add_select_fusion.place
  1.5 0.0 copy-start
  1.5 1.6 %copy-done = f32[16,8,32,128]{3,2,1,0:T(8,128)S(1)} copy-done((f32[16,8,32,128]{3,2,1,0:T(8,128)S(1)}, f32[16,8,32,128]{3,2,1,0:T(8,128)}, u32[]{:S(2)}) %copy-start) | copy-done | bytes 2097176
  3.1 0.0 copy-start.4
  3.1 0.8 copy-done.4
  3.8 0.0 copy-start.1
  3.8 0.0 copy-start.2
  3.8 0.0 copy-start.3
  3.8 11.2 %projector_table.1 = (bf16[256,96,128]{2,1,0:T(8,128)(2,1)S(1)}, f32[8,2,32,8,128]{4,3,2,1,0:T(8,128)S(1)}) custom-call(s32[8224]{0:T(1024)S(1)} %add_select_fusion.place, f32[8224]{0:T(1024)S(1)} %copy-done.4, f32[16,8,32,128]{3,2,1,0:T(8,128)S(1)} %copy-done), custom_call_target="tpu_custom_call" | custom-call | bytes 41943040 | tf_op jit(solution)/shard_map/projector_table/pallas_call | solution.py:107
  15.1 0.0 copy-done.5
  15.1 0.0 copy-done.6
  15.1 0.0 copy-done.1
  15.1 0.0 copy-done.2
  15.1 0.0 copy-done.3
  15.1 101.4 %bicg_solve.1 = (f32[8,2,32,8,128]{4,3,2,1,0:T(8,128)S(1)}, f32[8,8,128]{2,1,0:T(8,128)S(1)}) custom-call(bf16[256,96,128]{2,1,0:T(8,128)(2,1)S(1)} %get-tuple-element.6.table, f32[8,2,32,8,128]{4,3,2,1,0:T(8,128)S(1)} %get-tuple-element.7.orb, f32[256,128]{1,0:T(8,128)S(1)} %bitcast.5, f32[256,128]{1,0:T(8,128)S(1)} %bitcast.6, f32[16]{0:T(128)S(1)} %copy-done.6, ...), custom_call_target="tpu_custom_call" | custom-call | tf_op jit(solution)/shard_map/bicg_solve/pallas_call | solution.py:756
  116.5 1.7 %copy.11 = f32[2,8,8,32,128]{4,3,2,1,0:T(8,128)} copy(f32[2,8,8,32,128]{4,1,3,0,2:T(8,128)S(1)} %bitcast.4) | data formatting | bytes 4194304 | tf_op jit(solution)/shard_map/transpose | solution.py:814
  118.2 0.6 copy.13
Async XLA Ops:
  0.6 14.4 %copy-start.5 = (f32[1024]{0:T(1024)S(1)}, f32[1024]{0:T(1024)}, u32[]{:S(2)}) copy-start(f32[1024]{0:T(1024)} %kb.1) | copy-start | bytes 12292
  0.6 14.4 %copy-start.6 = (f32[16]{0:T(128)S(1)}, f32[16]{0:T(128)}, u32[]{:S(2)}) copy-start(f32[16]{0:T(128)} %lev.1) | copy-start | bytes 196
  1.5 1.6 %copy-start = (f32[16,8,32,128]{3,2,1,0:T(8,128)S(1)}, f32[16,8,32,128]{3,2,1,0:T(8,128)}, u32[]{:S(2)}) copy-start(f32[16,8,32,128]{3,2,1,0:T(8,128)} %orb.1) | copy-start | bytes 6291460
  3.1 0.8 copy-start.4
  3.8 11.2 %copy-start.1 = (f32[8,32,128]{2,1,0:T(8,128)S(1)}, f32[8,32,128]{2,1,0:T(8,128)}, u32[]{:S(2)}) copy-start(f32[8,32,128]{2,1,0:T(8,128)} %param.11) | copy-start | bytes 393220
  3.8 11.3 %copy-start.2 = (f32[8,32,128]{2,1,0:T(8,128)S(1)}, f32[8,32,128]{2,1,0:T(8,128)}, u32[]{:S(2)}) copy-start(f32[8,32,128]{2,1,0:T(8,128)} %param.12) | copy-start | bytes 393220
  3.8 11.3 %copy-start.3 = (bf16[256,256]{1,0:T(8,128)(2,1)S(1)}, bf16[256,256]{1,0:T(8,128)(2,1)}, u32[]{:S(2)}) copy-start(bf16[256,256]{1,0:T(8,128)(2,1)} %constant.25.clone.tz) | copy-start | bytes 393220
